TPU v7x, 1024 devices: a whole 4x8x16 slice. The times are simulated.
1024 devices in a mesh: ctx: 32 (over z, core), grp: 32 (over y, x).
Axes of the slice: x: 4, y: 8, z: 16, core: 2. Of those that a mesh axis runs over, the one named last changes fastest.
Arguments:
- queries: bfloat16 [1, 131072, 4096], P(None, ('ctx', 'grp')), may hold values from -200 to 200
- keyvals: bfloat16 [2, 1, 131072, 512], P(None, None, ('ctx', 'grp')), may hold values from -8 to 8
- seg_len: int32 [1, 512], replicated, may hold values from 128 to 384, as said below
- seg_task: int32 [1, 512], replicated, may hold values from 0 to 191
- task_slot: int32 [192], replicated, may hold values from 0 to 191, each once
- prefix_bank: bfloat16 [2, 192, 16, 512], P(None, 'grp'), may hold values from -9 to 9
Outputs:
- attended: bfloat16 [1, 131072, 4096], P(None, ('ctx', 'grp'))
Inputs may be any that keep to these rules, and one draw needn't show every extreme that they name: `seg_len`: the 512 lengths sum to 131072, and at least one equals 384. `task_slot`: A permutation; bank row r is held by index r // 6 of grp.
All inputs are finite; a program needn't handle non-finite values.
Results may differ from a plain program's by a relative error of at most 0.004.
Values may be sent and summed in bfloat16 or wider, within the bound.
A program may use at most 32 MiB of HBM per device.

v0:
```python
import math

import jax
import jax.numpy as jnp
from jax import lax
from jax.sharding import PartitionSpec as P

H = 32
KVH = 4
HD = 128
HOPS = 3


def shifted(block, axis, distance):
    devices = range(lax.axis_size(axis))
    route = [(i - distance, i) for i in devices if i - distance in devices]
    return lax.ppermute(block, axis, route)


def segment_index(starts, positions):
    return jnp.sum((starts[None, :] <= positions[:, None]).astype(jnp.int32), axis=1) - 1


def on_device(queries, keyvals, seg_len, seg_task, task_slot, prefix_bank):
    shard_len = queries.shape[1]
    groups = H // KVH
    feature_width = KVH * HD
    score_scale = 1.0 / math.sqrt(HD)
    grp_count = lax.axis_size("grp")
    shard_index = lax.axis_index("ctx") * grp_count + lax.axis_index("grp")
    task_dev = prefix_bank.shape[1]
    grouped_q = queries[0].reshape(shard_len, KVH, groups, HD)
    lengths = seg_len[0]
    row_tasks = seg_task[0]
    starts = jnp.cumsum(lengths) - lengths
    offsets = jnp.arange(shard_len, dtype=jnp.int32)
    query_pos = shard_index * shard_len + offsets
    query_seg = segment_index(starts, query_pos)

    def attend(carry_state, key_rows, value_rows, allowed):
        max_old, total_old, mixed_old = carry_state
        key_heads = key_rows.reshape(-1, KVH, HD)
        value_heads = value_rows.reshape(-1, KVH, HD)
        scores = (
            jnp.einsum("tkgd,skd->kgts", grouped_q, key_heads, preferred_element_type=jnp.float32)
            * score_scale
        )
        max_new = jnp.maximum(max_old, jnp.max(jnp.where(allowed, scores, -1e30), axis=-1))
        weights = jnp.where(allowed, jnp.exp(scores - max_new[..., None]), 0.0)
        shrink = jnp.exp(max_old - max_new)
        total_new = total_old * shrink + jnp.sum(weights, axis=-1)
        mixed_new = mixed_old * shrink[..., None] + jnp.einsum(
            "kgts,skd->kgtd",
            weights.astype(jnp.bfloat16),
            value_heads,
            preferred_element_type=jnp.float32,
        )
        return (max_new, total_new, mixed_new)

    start_state = (
        jnp.full((KVH, groups, shard_len), -1e30, jnp.float32),
        jnp.zeros((KVH, groups, shard_len), jnp.float32),
        jnp.zeros((KVH, groups, shard_len, HD), jnp.float32),
    )
    local_allowed = (query_seg[None, :] == query_seg[:, None]) & (
        query_pos[None, :] <= query_pos[:, None]
    )
    carry_state = attend(start_state, keyvals[0, 0], keyvals[1, 0], local_allowed)
    local_pair = keyvals[:, 0]
    kv_piece = local_pair
    for hop_count in range(1, HOPS + 1):
        kv_piece = shifted(kv_piece, ("ctx", "grp"), 1)
        key_pos = (shard_index - hop_count) * shard_len + offsets
        key_seg = segment_index(starts, key_pos)
        remote_allowed = query_seg[:, None] == key_seg[None, :]
        carry_state = attend(carry_state, kv_piece[0], kv_piece[1], remote_allowed)
    slot_seg = jnp.stack(
        [query_seg[0], jnp.where(query_seg[-1] != query_seg[0], query_seg[-1], -1)]
    )
    seg_pick = jnp.arange(row_tasks.shape[0])[None, :] == slot_seg[:, None]
    slot_task = jnp.sum(jnp.where(seg_pick, row_tasks[None, :], 0), axis=1)
    task_pick = jnp.arange(task_slot.shape[0])[None, :] == slot_task[:, None]
    bank_row = jnp.sum(jnp.where(task_pick, task_slot[None, :], 0), axis=1)
    owner_grp = bank_row // task_dev
    local_row = bank_row % task_dev
    slot_valid = slot_seg >= 0
    from_owner = jnp.arange(grp_count)[:, None] == owner_grp[None, :]
    requests = jnp.where(from_owner & slot_valid[None, :], local_row[None, :], -1)
    onehot = (
        lax.all_to_all(requests, "grp", split_axis=0, concat_axis=0, tiled=True)[..., None]
        == jnp.arange(task_dev)
    ).astype(jnp.bfloat16)
    bank_rows = jnp.einsum(
        "gnt,ctpf->gncpf", onehot, prefix_bank, preferred_element_type=jnp.float32
    ).astype(jnp.bfloat16)
    replies = lax.all_to_all(bank_rows, "grp", split_axis=0, concat_axis=0, tiled=True)
    fetched = jnp.sum(
        jnp.where(from_owner[:, :, None, None, None], replies.astype(jnp.float32), 0.0), axis=0
    ).astype(jnp.bfloat16)
    prefix_keys = fetched[:, 0].reshape(-1, feature_width)
    prefix_values = fetched[:, 1].reshape(-1, feature_width)
    prefix_seg = jnp.repeat(slot_seg, fetched.shape[2])
    prefix_allowed = query_seg[:, None] == prefix_seg[None, :]
    carry_state = attend(carry_state, prefix_keys, prefix_values, prefix_allowed)
    max_final, total_final, mixed_final = carry_state
    result = mixed_final / total_final[..., None]
    return result.transpose(2, 0, 1, 3).reshape(1, shard_len, H * HD).astype(jnp.bfloat16)


def solution(mesh):
    in_specs = (
        P(None, ("ctx", "grp"), None),
        P(None, None, ("ctx", "grp"), None),
        P(),
        P(),
        P(),
        P(None, "grp", None, None),
    )
    out_specs = P(None, ("ctx", "grp"), None)
    return jax.shard_map(
        on_device, mesh=mesh, in_specs=in_specs, out_specs=out_specs, check_vma=False
    )
```

profile of v0, /device:TPU:961, one launch (start us, length us, event | category | flops | bytes accessed | tf_op | source)
XLA Modules:
  0.0 145.8 jit_solution(1005136360309504404)
XLA Ops:
  0.0 1.0 reduce-window.9
  5.7 0.9 fusion.80
  6.6 0.9 fusion.82
  7.5 18.1 %all_to_all.11 = s32[32,1,2]{2,1,0:T(1,128)S(1)} all-to-all(s32[32,1,2]{2,1,0:T(1,128)S(1)} %and_select_fusion), channel_id=1, replica_groups=mesh['ctx'=32,'grp'=32] {'grp'}, dimensions={0} | all-to-all | bytes 512 | tf_op jit(solution)/shard_map/all_to_all | solution.py:90
  25.7 1.7 %convolution_convert_fusion = bf16[32,2,2,16,512]{4,0,3,2,1:T(8,128)(2,1)S(1)} fusion(bf16[2,6,16,512]{3,2,1,0:T(8,128)(2,1)} %param.11, s32[32,2]{0,1:T(2,128)S(1)} %bitcast.280), kind=kOutput, calls=%fused_computation.32 | convolution fusion | flops 13631872 | bytes 2294016 | tf_op jit(solution)/shard_map/gnt,ctpf->gncpf/dot_general | solution.py:93
  27.4 2.6 %copy.82 = bf16[32,2,2,16,512]{4,3,2,1,0:T(8,128)(2,1)} copy(bf16[32,2,2,16,512]{4,0,3,2,1:T(8,128)(2,1)S(1)} %convolution_convert_fusion) | data formatting | bytes 4194304 | tf_op jit(solution)/shard_map/convert_element_type | solution.py:95
  29.9 4.9 %all-to-all-start.1 = ((bf16[32,2,2,16,512]{4,3,2,1,0:T(8,128)(2,1)}), bf16[32,2,2,16,512]{4,3,2,1,0:T(8,128)(2,1)}, u32[]{:S(2)}, u32[]{:S(2)}) async-start(bf16[32,2,2,16,512]{4,3,2,1,0:T(8,128)(2,1)} %copy.82), calls=%async_computation.1 | async-start | bytes 4194304 | tf_op jit(solution)/shard_map/all_to_all | solution.py:96
  34.9 0.8 copy.70
  35.7 2.9 %collective-permute-start = (bf16[2,128,512]{1,2,0:T(8,128)(2,1)}, bf16[2,128,512]{1,2,0:T(8,128)(2,1)}, u32[]{:S(2)}, u32[]{:S(2)}) collective-permute-start(bf16[2,128,512]{1,2,0:T(8,128)(2,1)} %bitcast.11), channel_id=1, source_target_pairs={{0,1},{1,2},{2,3},{3,4},{4,5},{5,6},{6,7},{7,8},{8,9},{9,10},{10,1... | collective-permute-start | bytes 786440 | tf_op jit(solution)/shard_map/ppermute | solution.py:17
  39.1 0.7 compare_and_fusion
  39.8 1.3 fusion.15
  42.0 1.2 broadcast_compare_fusion.3
  43.2 53.5 %collective-permute-done = bf16[2,128,512]{1,2,0:T(8,128)(2,1)} collective-permute-done((bf16[2,128,512]{1,2,0:T(8,128)(2,1)}, bf16[2,128,512]{1,2,0:T(8,128)(2,1)}, u32[]{:S(2)}, u32[]{:S(2)}) %collective-permute-start) | collective-permute-done | bytes 262176 | tf_op jit(solution)/shard_map/ppermute | solution.py:17
  96.7 1.9 %collective-permute-start.1 = (bf16[2,128,512]{1,2,0:T(8,128)(2,1)}, bf16[2,128,512]{1,2,0:T(8,128)(2,1)S(1)}, u32[]{:S(2)}, u32[]{:S(2)}) collective-permute-start(bf16[2,128,512]{1,2,0:T(8,128)(2,1)} %collective-permute-done), channel_id=1, source_target_pairs={{0,1},{1,2},{2,3},{3,4},{4,5},{5,6},{6,7},{7,8},{8,9},{9,10},{10,1... | collective-permute-start | bytes 786440 | tf_op jit(solution)/shard_map/ppermute | solution.py:17
  98.6 1.0 fusion.98
  99.6 2.6 %fusion.11 = (f32[4,8,128]{2,1,0:T(8,128)}, f32[4,128,128,8]{2,1,3,0:T(8,128)}) fusion(pred[128,128]{0,1:T(8,128)(4,1)S(1)} %get-tuple-element.35, bf16[128,4,128,1]{0,2,3,1:T(8,128)(2,1)S(1)} %bitcast.272, bf16[128,4,8,128]{3,2,1,0:T(8,128)(2,1)S(1)} %bitcast.261), kind=kOutput, calls=%fused_computation.22 | convolution fusion | flops 135786496 | bytes 3309568 | tf_op jit(solution)/shard_map/tkgd,skd->kgts/dot_general | solution.py:45
  102.2 5.7 %collective-permute-done.1 = bf16[2,128,512]{1,2,0:T(8,128)(2,1)S(1)} collective-permute-done((bf16[2,128,512]{1,2,0:T(8,128)(2,1)}, bf16[2,128,512]{1,2,0:T(8,128)(2,1)S(1)}, u32[]{:S(2)}, u32[]{:S(2)}) %collective-permute-start.1) | collective-permute-done | bytes 262176 | tf_op jit(solution)/shard_map/ppermute | solution.py:17
  107.9 2.1 %collective-permute-start.2 = (bf16[2,128,512]{1,2,0:T(8,128)(2,1)S(1)}, bf16[2,128,512]{1,2,0:T(8,128)(2,1)S(1)}, u32[]{:S(2)}, u32[]{:S(2)}) collective-permute-start(bf16[2,128,512]{1,2,0:T(8,128)(2,1)S(1)} %collective-permute-done.1), channel_id=1, source_target_pairs={{0,1},{1,2},{2,3},{3,4},{4,5},{5,6},{6,7},{7,8},{8,9},{9,10},{10,1... | collective-permute-start | bytes 786440 | tf_op jit(solution)/shard_map/ppermute | solution.py:17
  110.0 2.5 %fusion.7 = (f32[4,8,128]{2,1,0:T(8,128)}, f32[4,128,128,8]{2,1,3,0:T(8,128)}) fusion(pred[128,128]{0,1:T(8,128)(4,1)S(1)} %get-tuple-element.33, bf16[128,4,128,1]{0,2,3,1:T(8,128)(2,1)S(1)} %bitcast.273, bf16[128,4,8,128]{3,2,1,0:T(8,128)(2,1)S(1)} %bitcast.262), kind=kOutput, calls=%fused_computation.15 | convolution fusion | flops 135786496 | bytes 3309568 | tf_op jit(solution)/shard_map/tkgd,skd->kgts/dot_general | solution.py:45
  112.6 6.3 %collective-permute-done.2 = bf16[2,128,512]{1,2,0:T(8,128)(2,1)S(1)} collective-permute-done((bf16[2,128,512]{1,2,0:T(8,128)(2,1)S(1)}, bf16[2,128,512]{1,2,0:T(8,128)(2,1)S(1)}, u32[]{:S(2)}, u32[]{:S(2)}) %collective-permute-start.2) | collective-permute-done | bytes 262176 | tf_op jit(solution)/shard_map/ppermute | solution.py:17
  119.6 2.6 %fusion.3 = (f32[4,8,128]{2,1,0:T(8,128)}, f32[4,128,128,8]{2,1,3,0:T(8,128)}) fusion(pred[128,128]{0,1:T(8,128)(4,1)S(1)} %copy-done.11, bf16[128,4,128,1]{0,2,3,1:T(8,128)(2,1)S(1)} %bitcast.271, bf16[128,4,8,128]{3,2,1,0:T(8,128)(2,1)S(1)} %bitcast.263), kind=kOutput, calls=%fused_computation.8 | convolution fusion | flops 135786496 | bytes 3309568 | tf_op jit(solution)/shard_map/tkgd,skd->kgts/dot_general | solution.py:45
  122.2 2.1 %select_reduce_fusion = bf16[2,2,16,512]{3,2,1,0:T(8,128)(2,1)S(1)} fusion(bf16[32,2,2,16,512]{4,3,2,1,0:T(8,128)(2,1)} %all-to-all-done.1, pred[32,2]{1,0:T(8,128)(4,1)} %iota_compare_fusion), kind=kLoop, calls=%fused_computation | loop fusion | flops 3112960 | bytes 2162752 | tf_op jit(solution)/shard_map/reduce_sum | solution.py:97
  124.9 1.4 reshape_reshape_squeeze.6
  126.3 2.1 %select_reduce_fusion.1 = (f32[4,8,128]{2,1,0:T(8,128)S(1)}, f32[4,8,128,32]{2,3,1,0:T(8,128)}) fusion(pred[128,32]{0,1:T(8,128)(4,1)} %broadcast_compare_fusion.3, bf16[128,4,8,128]{3,2,1,0:T(8,128)(2,1)S(1)} %bitcast.264, bf16[32,4,128,1]{2,1,0,3:T(4,128)(2,1)} %bitcast.274), kind=kOutput, calls=%fused_computation.72 | convolution fusion | flops 33943552 | bytes 1626112 | tf_op jit(solution)/shard_map/tkgd,skd->kgts/dot_general | solution.py:45
  129.0 1.4 fusion.94
  130.3 1.8 %fusion.18 = f32[4,8,128]{2,1,0:T(8,128)} fusion(f32[4,128,128,8]{2,1,3,0:T(8,128)S(1)} %get-tuple-element.49, f32[4,8,128]{2,1,0:T(8,128)S(1)} %get-tuple-element.31, pred[128,128]{0,1:T(8,128)(4,1)} %copy-done.9), kind=kLoop, calls=%fused_computation.33 | loop fusion | flops 2093056 | bytes 2146304 | tf_op jit(solution)/shard_map/reduce_sum | solution.py:51
  132.1 1.9 %fusion.32 = f32[4,8,128,128]{2,3,1,0:T(8,128)} fusion(bf16[128,4,128,1]{0,2,3,1:T(8,128)(2,1)S(1)} %bitcast.267, f32[4,128,128,8]{2,1,3,0:T(8,128)S(1)} %get-tuple-element.49, f32[4,8,128]{2,1,0:T(8,128)S(1)} %get-tuple-element.31, pred[128,128]{0,1:T(8,128)(4,1)S(1)} %copy-done.10), kind=kOutput, calls=%fused_computation.45 | convolution fusion | flops 136314880 | bytes 4358144 | tf_op jit(solution)/shard_map/kgts,skd->kgtd/dot_general | solution.py:52
  134.5 1.9 %fusion.30 = f32[4,8,128,128]{2,3,1,0:T(8,128)} fusion(bf16[128,4,128,1]{0,2,3,1:T(8,128)(2,1)S(1)} %bitcast.269, f32[4,128,128,8]{2,1,3,0:T(8,128)S(1)} %copy-done, f32[4,8,128]{2,1,0:T(8,128)S(1)} %get-tuple-element.16, pred[128,128]{0,1:T(8,128)(4,1)S(1)} %copy-done.8), kind=kOutput, calls=%fused_computation.44 | convolution fusion | flops 136314880 | bytes 4358144 | tf_op jit(solution)/shard_map/kgts,skd->kgtd/dot_general | solution.py:52
  136.8 1.8 %fusion.28 = f32[4,8,128,128]{2,3,1,0:T(8,128)} fusion(bf16[128,4,128,1]{0,2,3,1:T(8,128)(2,1)S(1)} %bitcast.270, f32[4,128,128,8]{2,1,3,0:T(8,128)S(1)} %copy-done.1, f32[4,8,128]{2,1,0:T(8,128)S(1)} %get-tuple-element.15, pred[128,128]{0,1:T(8,128)(4,1)S(1)} %get-tuple-element.33), kind=kOutput, calls=%fused_computation.43 | convolution fusion | flops 136314880 | bytes 4358144 | tf_op jit(solution)/shard_map/kgts,skd->kgtd/dot_general | solution.py:52
  139.4 0.8 copy-done.2
  141.1 3.4 %fusion.1 = bf16[128,4,8,128]{0,3,2,1:T(8,128)(2,1)S(1)} fusion(f32[4,8,128,128]{2,3,1,0:T(8,128)S(1)} %fusion.61, f32[4,8,128,128]{2,3,1,0:T(8,128)} %fusion.28, f32[4,8,128,128]{2,3,1,0:T(8,128)} %fusion.30, f32[4,8,128,128]{2,3,1,0:T(8,128)S(1)} %copy-done.4, bf16[128,4,128,1]{0,2,3,1:T(8,128)(2,1)S(1)} %bitcast.275, ...), kind=kOutput, calls=%fused_computation.3 | convolution fusion | flops 142082048 | bytes 11796480 | tf_op jit(solution)/shard_map/kgts,skd->kgtd/dot_general | solution.py:52
  144.5 1.3 copy.87
  (86 shorter events, 8.4 us)
Async XLA Ops:
  2.3 36.8 %copy-start.25 = (s32[128]{0:T(128)}, s32[128]{0:T(128)S(1)}, u32[]{:S(2)}) copy-start(s32[128]{0:T(128)S(1)} %get-tuple-element.53) | copy-start | bytes 1540
  29.9 4.9 %copy-start.6 = (bf16[2,1,128,512]{3,2,1,0:T(8,128)(2,1)S(1)}, bf16[2,1,128,512]{3,2,1,0:T(8,128)(2,1)}, u32[]{:S(2)}) copy-start(bf16[2,1,128,512]{3,2,1,0:T(8,128)(2,1)} %param.7) | copy-start | bytes 786436
  29.9 8.7 %copy-start.5 = (bf16[1,128,4096]{2,1,0:T(8,128)(2,1)S(1)}, bf16[1,128,4096]{2,1,0:T(8,128)(2,1)}, u32[]{:S(2)}) copy-start(bf16[1,128,4096]{2,1,0:T(8,128)(2,1)} %param.6) | copy-start | bytes 3145732
  29.9 92.2 %all-to-all-start.1 = ((bf16[32,2,2,16,512]{4,3,2,1,0:T(8,128)(2,1)}), bf16[32,2,2,16,512]{4,3,2,1,0:T(8,128)(2,1)}, u32[]{:S(2)}, u32[]{:S(2)}) async-start(bf16[32,2,2,16,512]{4,3,2,1,0:T(8,128)(2,1)} %copy.82), calls=%async_computation.1 | async-start | bytes 4194304 | tf_op jit(solution)/shard_map/all_to_all | solution.py:96
  35.7 61.0 %collective-permute-start = (bf16[2,128,512]{1,2,0:T(8,128)(2,1)}, bf16[2,128,512]{1,2,0:T(8,128)(2,1)}, u32[]{:S(2)}, u32[]{:S(2)}) collective-permute-start(bf16[2,128,512]{1,2,0:T(8,128)(2,1)} %bitcast.11), channel_id=1, source_target_pairs={{0,1},{1,2},{2,3},{3,4},{4,5},{5,6},{6,7},{7,8},{8,9},{9,10},{10,1... | collective-permute-start | bytes 786440 | tf_op jit(solution)/shard_map/ppermute | solution.py:17
  39.8 1.3 copy-start.9
  39.8 62.4 %copy-start.7 = (pred[128,128]{0,1:T(8,128)(4,1)}, pred[128,128]{0,1:T(8,128)(4,1)S(1)}, u32[]{:S(2)}) copy-start(pred[128,128]{0,1:T(8,128)(4,1)S(1)} %get-tuple-element.35) | copy-start | bytes 49156
  96.7 11.2 %collective-permute-start.1 = (bf16[2,128,512]{1,2,0:T(8,128)(2,1)}, bf16[2,128,512]{1,2,0:T(8,128)(2,1)S(1)}, u32[]{:S(2)}, u32[]{:S(2)}) collective-permute-start(bf16[2,128,512]{1,2,0:T(8,128)(2,1)} %collective-permute-done), channel_id=1, source_target_pairs={{0,1},{1,2},{2,3},{3,4},{4,5},{5,6},{6,7},{7,8},{8,9},{9,10},{10,1... | collective-permute-start | bytes 786440 | tf_op jit(solution)/shard_map/ppermute | solution.py:17
  102.2 17.4 %copy-start.11 = (pred[128,128]{0,1:T(8,128)(4,1)S(1)}, pred[128,128]{0,1:T(8,128)(4,1)}, u32[]{:S(2)}) copy-start(pred[128,128]{0,1:T(8,128)(4,1)} %get-tuple-element.34) | copy-start | bytes 49156
  107.9 11.0 %collective-permute-start.2 = (bf16[2,128,512]{1,2,0:T(8,128)(2,1)S(1)}, bf16[2,128,512]{1,2,0:T(8,128)(2,1)S(1)}, u32[]{:S(2)}, u32[]{:S(2)}) collective-permute-start(bf16[2,128,512]{1,2,0:T(8,128)(2,1)S(1)} %collective-permute-done.1), channel_id=1, source_target_pairs={{0,1},{1,2},{2,3},{3,4},{4,5},{5,6},{6,7},{7,8},{8,9},{9,10},{10,1... | collective-permute-start | bytes 786440 | tf_op jit(solution)/shard_map/ppermute | solution.py:17
  126.3 5.9 %copy-start.10 = (pred[128,128]{0,1:T(8,128)(4,1)S(1)}, pred[128,128]{0,1:T(8,128)(4,1)}, u32[]{:S(2)}) copy-start(pred[128,128]{0,1:T(8,128)(4,1)} %copy-done.9) | copy-start | bytes 49156
  128.4 0.6 copy-start.17
  132.1 1.9 %copy-start = (f32[4,128,128,8]{2,1,3,0:T(8,128)S(1)}, f32[4,128,128,8]{2,1,3,0:T(8,128)}, u32[]{:S(2)}) copy-start(f32[4,128,128,8]{2,1,3,0:T(8,128)} %get-tuple-element.47) | copy-start | bytes 6291460
  132.1 1.9 %copy-start.8 = (pred[128,128]{0,1:T(8,128)(4,1)S(1)}, pred[128,128]{0,1:T(8,128)(4,1)}, u32[]{:S(2)}) copy-start(pred[128,128]{0,1:T(8,128)(4,1)} %copy-done.7) | copy-start | bytes 49156
  134.5 1.9 %copy-start.1 = (f32[4,128,128,8]{2,1,3,0:T(8,128)S(1)}, f32[4,128,128,8]{2,1,3,0:T(8,128)}, u32[]{:S(2)}) copy-start(f32[4,128,128,8]{2,1,3,0:T(8,128)} %get-tuple-element.45) | copy-start | bytes 6291460
  136.8 1.9 %copy-start.20 = (bf16[2,1,16,512]{3,2,1,0:T(8,128)(2,1)S(1)}, bf16[2,1,16,512]{3,2,1,0:T(8,128)(2,1)}, u32[]{:S(2)}) copy-start(bf16[2,1,16,512]{3,2,1,0:T(8,128)(2,1)} %get-tuple-element.27) | copy-start | bytes 98308
  136.8 1.9 %copy-start.3 = (f32[4,8,128,32]{2,3,1,0:T(8,128)S(1)}, f32[4,8,128,32]{2,3,1,0:T(8,128)}, u32[]{:S(2)}) copy-start(f32[4,8,128,32]{2,3,1,0:T(8,128)} %get-tuple-element.41) | copy-start | bytes 1572868
  136.8 1.9 %copy-start.19 = (f32[4,8,128]{2,1,0:T(8,128)S(1)}, f32[4,8,128]{2,1,0:T(8,128)}, u32[]{:S(2)}) copy-start(f32[4,8,128]{2,1,0:T(8,128)} %get-tuple-element.13) | copy-start | bytes 49156
  136.8 1.9 %copy-start.22 = (pred[128,32]{0,1:T(8,128)(4,1)S(1)}, pred[128,32]{0,1:T(8,128)(4,1)}, u32[]{:S(2)}) copy-start(pred[128,32]{0,1:T(8,128)(4,1)} %broadcast_compare_fusion.3) | copy-start | bytes 12292
  138.7 1.6 %copy-start.2 = (f32[4,128,128,8]{2,1,3,0:T(8,128)S(1)}, f32[4,128,128,8]{2,1,3,0:T(8,128)}, u32[]{:S(2)}) copy-start(f32[4,128,128,8]{2,1,3,0:T(8,128)} %get-tuple-element.43) | copy-start | bytes 6291460
  138.7 1.6 %copy-start.12 = (pred[128,128]{0,1:T(8,128)(4,1)S(1)}, pred[128,128]{0,1:T(8,128)(4,1)}, u32[]{:S(2)}) copy-start(pred[128,128]{0,1:T(8,128)(4,1)} %get-tuple-element.34) | copy-start | bytes 49156
  138.7 1.6 %copy-start.23 = (f32[4,8,128]{2,1,0:T(8,128)S(1)}, f32[4,8,128]{2,1,0:T(8,128)}, u32[]{:S(2)}) copy-start(f32[4,8,128]{2,1,0:T(8,128)} %get-tuple-element.14) | copy-start | bytes 49156
  138.9 1.9 %copy-start.13 = (f32[4,8,128]{2,1,0:T(8,128)S(1)}, f32[4,8,128]{2,1,0:T(8,128)}, u32[]{:S(2)}) copy-start(f32[4,8,128]{2,1,0:T(8,128)} %get-tuple-element.48) | copy-start | bytes 49156
  138.9 1.9 %copy-start.14 = (f32[4,8,128]{2,1,0:T(8,128)S(1)}, f32[4,8,128]{2,1,0:T(8,128)}, u32[]{:S(2)}) copy-start(f32[4,8,128]{2,1,0:T(8,128)} %get-tuple-element.46) | copy-start | bytes 49156
  138.9 1.9 %copy-start.15 = (f32[4,8,128]{2,1,0:T(8,128)S(1)}, f32[4,8,128]{2,1,0:T(8,128)}, u32[]{:S(2)}) copy-start(f32[4,8,128]{2,1,0:T(8,128)} %get-tuple-element.44) | copy-start | bytes 49156
  138.9 1.9 %copy-start.16 = (f32[4,8,128]{2,1,0:T(8,128)S(1)}, f32[4,8,128]{2,1,0:T(8,128)}, u32[]{:S(2)}) copy-start(f32[4,8,128]{2,1,0:T(8,128)} %get-tuple-element.42) | copy-start | bytes 49156
  138.9 1.9 %copy-start.18 = (f32[4,8,128]{2,1,0:T(8,128)S(1)}, f32[4,8,128]{2,1,0:T(8,128)}, u32[]{:S(2)}) copy-start(f32[4,8,128]{2,1,0:T(8,128)} %copy-done.17) | copy-start | bytes 49156
  138.9 1.9 %copy-start.24 = (f32[4,8,128]{2,1,0:T(8,128)S(1)}, f32[4,8,128]{2,1,0:T(8,128)}, u32[]{:S(2)}) copy-start(f32[4,8,128]{2,1,0:T(8,128)} %fusion.18) | copy-start | bytes 49156
  138.9 2.1 %copy-start.4 = (f32[4,8,128,128]{2,3,1,0:T(8,128)S(1)}, f32[4,8,128,128]{2,3,1,0:T(8,128)}, u32[]{:S(2)}) copy-start(f32[4,8,128,128]{2,3,1,0:T(8,128)} %fusion.32) | copy-start | bytes 6291460
  138.9 2.1 %copy-start.21 = (bf16[1,128,512]{1,2,0:T(8,128)(2,1)S(1)}, bf16[1,128,512]{1,2,0:T(8,128)(2,1)}, u32[]{:S(2)}) copy-start(bf16[1,128,512]{1,2,0:T(8,128)(2,1)} %get-tuple-element.19) | copy-start | bytes 393220
where the time goes:
time: 147 us; the launch traced here: 146 us
  waiting for transfers between devices  65.6 us (45%)
  matrix products  22.1 us (15%)
  blocking collectives  18.1 us (12%)
  other arithmetic  14 us (10%)
  local copies, waits for them, and re-layouts  11.8 us (8%)
  starting transfers between devices  11.8 us (8%)
  between operations  2.45 us (2%)
    ppermute x3, waiting for transfers between devices, shifted(): return lax.ppermute(block, axis, route)  65.6 us
    all_to_all x1, blocking collectives, on_device(): lax.all_to_all(requests, 'grp', split_axis=0, concat_axis=0, tiled=True)  18.1 us
    dot_general x5, matrix products, attend(): jnp.einsum('tkgd,skd->kgts', grouped_q, key_heads, preferred_element_type...  11 us
    dot_general x5, matrix products, attend(): jnp.einsum('kgts,skd->kgtd', weights.astype(jnp.bfloat16), value_heads, p...  9.4 us
    ppermute x3, starting transfers between devices, shifted(): return lax.ppermute(block, axis, route)  6.94 us
    all_to_all x1, starting transfers between devices, on_device(): lax.all_to_all(bank_rows, 'grp', split_axis=0, concat_axis=0, tiled=True)  4.89 us
    reduce_sum x5, other arithmetic, attend(): total_new = total_old * shrink + jnp.sum(weights, axis=-1)  3.32 us
    unnamed x55, local copies, waits for them, and re-layouts  2.97 us
  transfers between devices with their start and end apart: 4, of which 3 were waited for; matrix products, arithmetic and copies ran while one was open for 10% of the time, Pallas kernels for 0%

commit v1 on v0

v1 whole, which is shorter than its diff:
```python
import math

import jax
import jax.numpy as jnp
from jax import lax
from jax.experimental import pallas as pl
from jax.experimental.pallas import tpu as pltpu
from jax.sharding import PartitionSpec as P

H = 32
KVH = 4
HD = 128
GROUPS = H // KVH
T = 128
PREFIX = 16
SEGS = 512
ROWS6 = 6
HALF = ROWS6 // 2
NX = 4
NY = 8
KEYS = 4 * T
SLOTS = KEYS + 2 * PREFIX
EXP_SCALE = math.log2(math.e) / math.sqrt(HD)
NEG = -1e30
BIG = 1 << 30


def scan_lanes(row):
    lane = lax.broadcasted_iota(jnp.int32, row.shape, 1)
    step = 1
    while step < row.shape[1]:
        row = row + jnp.where(lane >= step, pltpu.roll(row, step, 1), 0)
        step *= 2
    return row


def kernel(
    q_hbm,
    kv_hbm,
    len_hbm,
    task_hbm,
    slot_smem,
    bank_hbm,
    out_hbm,
    q_buf,
    kv_buf,
    pass_buf,
    col_bank,
    pick_out,
    pick_in,
    acc_buf,
    max_buf,
    bias_buf,
    pbias_buf,
    out_buf,
    len_buf,
    task_buf,
    local_sem,
    out_sem,
    kv_send,
    kv_recv,
    ring_send,
    ring_recv,
    sib_send,
    sib_recv,
    pick_send,
    pick_recv,
):
    ctx = lax.axis_index("ctx")
    grp = lax.axis_index("grp")
    n_ctx = lax.axis_size("ctx")
    core = ctx % 2
    x = grp % NX
    y = grp // NX
    shard = ctx * (NX * NY) + grp

    next_ctx = jnp.where(y == NY - 1, (ctx + 1) % n_ctx, ctx)
    prev_ctx = jnp.where(y == 0, (ctx + n_ctx - 1) % n_ctx, ctx)
    up = (y + 1) % NY
    down = (y + NY - 1) % NY

    def in_row(col):
        return {"ctx": ctx, "grp": y * NX + col}

    def in_next(col):
        return {"ctx": next_ctx, "grp": up * NX + col}

    def in_prev(col):
        return {"ctx": prev_ctx, "grp": down * NX + col}

    ring_up = {"ctx": ctx, "grp": up * NX + x}
    ring_down = {"ctx": ctx, "grp": down * NX + x}
    sibling = {"ctx": ctx + 1 - 2 * core, "grp": grp}

    kv_local = []
    for j in range(KVH):
        copy = pltpu.make_async_copy(
            kv_hbm.at[:, 0, :, pl.ds(j * HD, HD)],
            kv_buf.at[j, :, pl.ds(0, T), :],
            local_sem.at[j],
        )
        copy.start()
        kv_local.append(copy)
    bank_local = pltpu.make_async_copy(bank_hbm, col_bank.at[y], local_sem.at[4])
    bank_local.start()
    len_copy = pltpu.make_async_copy(len_hbm, len_buf, local_sem.at[5])
    len_copy.start()
    task_copy = pltpu.make_async_copy(task_hbm, task_buf, local_sem.at[6])
    task_copy.start()
    q_copy = pltpu.make_async_copy(q_hbm.at[0], q_buf, local_sem.at[7])
    q_copy.start()

    barrier = pltpu.get_barrier_semaphore()

    def greet(device):
        pl.semaphore_signal(barrier, inc=1, device_id=device, device_id_type=pl.DeviceIdType.MESH)

    for hop in range(1, NX):
        greet(in_row((x + hop) % NX))
    greet(ring_up)
    greet(ring_down)
    greet(sibling)

    @pl.when(y == NY - 1)
    def _():
        greet(in_next(x))

    @pl.when(y == 0)
    def _():
        greet(in_prev(x))

    @pl.when(x == 0)
    def _():
        greet(in_prev(NX - 1))

    @pl.when(x == NX - 1)
    def _():
        greet(in_next(0))

    edge_y = jnp.where((y == 0) | (y == NY - 1), 1, 0)
    edge_x = jnp.where((x == 0) | (x == NX - 1), 1, 0)
    pl.semaphore_wait(barrier, 6 + edge_y + edge_x)

    def slot_ref(j, slot):
        if slot == 4:
            return pass_buf.at[j]
        return kv_buf.at[j, :, pl.ds(slot * T, T), :]

    def kv_copy(j, number, source, device, target):
        return pltpu.make_async_remote_copy(
            src_ref=slot_ref(j, source),
            dst_ref=slot_ref(j, target),
            send_sem=kv_send.at[number, j],
            recv_sem=kv_recv.at[target - 1, j],
            device_id=device,
            device_id_type=pl.DeviceIdType.MESH,
        )

    def wait_kv(j, slot):
        kv_copy(j, 0, slot, sibling, slot).wait_recv()

    def ring_copy(number, owner, device):
        piece = col_bank.at[owner, :, pl.ds(HALF * core, HALF)]
        return pltpu.make_async_remote_copy(
            src_ref=piece,
            dst_ref=piece,
            send_sem=ring_send.at[number],
            recv_sem=ring_recv.at[number],
            device_id=device,
            device_id_type=pl.DeviceIdType.MESH,
        )

    def sib_copy(number, owner, half):
        piece = col_bank.at[owner, :, pl.ds(HALF * half, HALF)]
        return pltpu.make_async_remote_copy(
            src_ref=piece,
            dst_ref=piece,
            send_sem=sib_send.at[number],
            recv_sem=sib_recv.at[number],
            device_id=sibling,
            device_id_type=pl.DeviceIdType.MESH,
        )

    def down_copy(step):
        return ring_copy(step, (y + step) % NY, ring_down)

    def up_copy(step):
        return ring_copy(4 + step, (y + NY - step) % NY, ring_up)

    bank_local.wait()
    down_copy(0).start()
    up_copy(0).start()
    for j in range(KVH):
        kv_local[j].wait()

        @pl.when(x < NX - 1)
        def _():
            kv_copy(j, 0, 0, in_row((x + 1) % NX), 1).start()

        @pl.when(x > 0)
        def _():
            kv_copy(j, 1, 0, in_next(x), 4).start()

        @pl.when(x == 0)
        def _():
            kv_copy(j, 1, 0, in_row(NX - 1), 3).start()

    len_copy.wait()
    task_copy.wait()
    lengths = len_buf[...]
    starts = scan_lanes(lengths) - lengths
    tasks = task_buf[...]

    def segments(first):
        start_a = jnp.max(jnp.where(starts <= first, starts, 0))
        start_b = jnp.min(jnp.where(starts > first, starts, BIG))
        return start_a, start_b

    def bank_row(start):
        task = jnp.sum(jnp.where(starts == start, tasks, 0))
        row = slot_smem[task]
        owner = (row * 10923) >> 16
        return owner % NX, owner // NX, row - ROWS6 * owner

    here_a, here_b = segments(shard * T)
    rel_a = here_a - shard * T
    rel_b = here_b - shard * T

    query_at = lax.broadcasted_iota(jnp.int32, (T, KEYS), 0)
    column = lax.broadcasted_iota(jnp.int32, (T, KEYS), 1)
    key_at = (column % T) - (column // T) * T
    earliest = jnp.where(query_at < rel_b, rel_a, rel_b)
    bias_buf[...] = jnp.where((key_at >= earliest) & (key_at <= query_at), 0.0, NEG)
    query_at = lax.broadcasted_iota(jnp.int32, (T, 2 * PREFIX), 0)
    column = lax.broadcasted_iota(jnp.int32, (T, 2 * PREFIX), 1)
    pbias_buf[...] = jnp.where((query_at < rel_b) == (column < PREFIX), 0.0, NEG)

    q_copy.wait()
    ones = jnp.ones((KEYS, HD), jnp.bfloat16)
    row_parity = core
    next_parity = next_ctx % 2
    prev_parity = prev_ctx % 2

    def relay(j):
        @pl.when(x > 0)
        def _():
            wait_kv(j, 4)

        @pl.when((x == 1) | (x == 2))
        def _():
            kv_copy(j, 2, 4, in_row(x - 1), 3).start()

        @pl.when(x == 3)
        def _():
            kv_copy(j, 2, 4, in_row(2), 3).start()
            kv_copy(j, 3, 4, in_row(0), 1).start()

        wait_kv(j, 1)

        @pl.when((row_parity == 0) & ((x == 1) | (x == 2)))
        def _():
            kv_copy(j, 3, 1, in_row(x + 1), 2).start()

        @pl.when((row_parity == 1) & (x == 0))
        def _():
            kv_copy(j, 2, 1, in_row(1), 2).start()

        @pl.when((x == 3) & (next_parity == 1))
        def _():
            kv_copy(j, 4, 1, in_next(0), 2).start()

        wait_kv(j, 3)

        @pl.when((row_parity == 0) & ((x == 1) | (x == 2)))
        def _():
            kv_copy(j, 4, 3, in_row(x - 1), 2).start()

        @pl.when((row_parity == 1) & (x == 3))
        def _():
            kv_copy(j, 5, 3, in_row(2), 2).start()

        @pl.when((x == 0) & (prev_parity == 1))
        def _():
            kv_copy(j, 3, 3, in_prev(NX - 1), 2).start()

        wait_kv(j, 2)

    def row_keys(j):
        keys = kv_buf[j, 0, pl.ds(0, KEYS), :]
        values = jnp.concatenate([kv_buf[j, 1, pl.ds(0, KEYS), :], ones], axis=1)
        for g in range(GROUPS):
            query = q_buf[:, pl.ds(pl.multiple_of((j * GROUPS + g) * HD, HD), HD)]
            scores = lax.dot_general(
                query, keys, (((1,), (1,)), ((), ())), preferred_element_type=jnp.float32
            )
            scores = scores + bias_buf[...]
            top = jnp.max(scores, axis=1, keepdims=True)
            weights = jnp.exp2((scores - top) * EXP_SCALE).astype(jnp.bfloat16)
            acc_buf[j, g] = jnp.dot(weights, values, preferred_element_type=jnp.float32)
            max_buf[j, g] = jnp.broadcast_to(top, (T, HD))

    def ring_step(step):
        ring_copy(step, (y + 1 + step) % NY, ring_down).wait_recv()
        if step < 3:
            down_copy(step + 1).start()
        sib_copy(step, (y + 1 + step) % NY, core).start()
        if step < 3:
            ring_copy(4 + step, (y + NY - 1 - step) % NY, ring_up).wait_recv()
            if step < 2:
                up_copy(step + 1).start()
            sib_copy(4 + step, (y + NY - 1 - step) % NY, core).start()

    for j in range(KVH):
        ring_step(j)
        relay(j)
        row_keys(j)

    for step in range(4):
        sib_copy(step, (y + 1 + step) % NY, 1 - core).wait_recv()
    for step in range(3):
        sib_copy(4 + step, (y + NY - 1 - step) % NY, 1 - core).wait_recv()

    def pick(col):
        first = (shard - x + col) * T
        start_a, start_b = segments(first)
        rows = []
        for start in (start_a, start_b):
            _, owner_y, row = bank_row(start)
            rows.append(col_bank[owner_y, :, row])
        return rows

    def pick_copy(hop, col):
        return pltpu.make_async_remote_copy(
            src_ref=pick_out.at[hop - 1],
            dst_ref=pick_in.at[hop],
            send_sem=pick_send.at[hop - 1],
            recv_sem=pick_recv.at[hop - 1],
            device_id=in_row(col),
            device_id_type=pl.DeviceIdType.MESH,
        )

    for hop in (2, 1, 3):
        col = (x + hop) % NX
        rows = pick(col)
        pick_out[hop - 1, 0] = rows[0]
        pick_out[hop - 1, 1] = rows[1]
        pick_copy(hop, col).start()
    rows = pick(x)
    pick_in[0, 0] = rows[0]
    pick_in[0, 1] = rows[1]
    for hop in range(1, NX):
        pick_copy(hop, (x + hop) % NX).wait_recv()
    for which, start in enumerate((here_a, here_b)):
        owner_x, _, _ = bank_row(start)
        row = pick_in[(x + NX - owner_x) % NX, which]
        for j in range(KVH):
            for part in range(2):
                kv_buf[j, part, pl.ds(KEYS + which * PREFIX, PREFIX), :] = row[
                    part, :, j * HD : (j + 1) * HD
                ]

    short_ones = jnp.ones((2 * PREFIX, HD), jnp.bfloat16)
    out_copies = []
    for j in range(KVH):
        keys = kv_buf[j, 0, pl.ds(KEYS, 2 * PREFIX), :]
        values = jnp.concatenate([kv_buf[j, 1, pl.ds(KEYS, 2 * PREFIX), :], short_ones], axis=1)
        for g in range(GROUPS):
            query = q_buf[:, pl.ds((j * GROUPS + g) * HD, HD)]
            scores = lax.dot_general(
                query, keys, (((1,), (1,)), ((), ())), preferred_element_type=jnp.float32
            )
            scores = scores + pbias_buf[...]
            old_top = max_buf[j, g]
            top = jnp.maximum(old_top, jnp.max(scores, axis=1, keepdims=True))
            shrink = jnp.exp2((old_top - top) * EXP_SCALE)
            weights = jnp.exp2((scores - top[:, : 2 * PREFIX]) * EXP_SCALE).astype(jnp.bfloat16)
            fresh = jnp.dot(weights, values, preferred_element_type=jnp.float32)
            mixed = acc_buf[j, g, :, pl.ds(0, HD)] * shrink + fresh[:, :HD]
            total = acc_buf[j, g, :, pl.ds(HD, HD)] * shrink + fresh[:, HD:]
            out_buf[:, pl.ds((j * GROUPS + g) * HD, HD)] = (mixed / total).astype(jnp.bfloat16)
        span = pl.ds(j * GROUPS * HD, GROUPS * HD)
        copy = pltpu.make_async_copy(out_buf.at[:, span], out_hbm.at[0, :, span], out_sem.at[j])
        copy.start()
        out_copies.append(copy)

    for j in range(KVH):

        def sent(number, j=j):
            kv_copy(j, number, 0, sibling, 1).wait_send()

        @pl.when(x < NX - 1)
        def _():
            sent(0)

        sent(1)

        @pl.when(x > 0)
        def _():
            sent(2)

        @pl.when(x == 3)
        def _():
            sent(3)

        @pl.when((row_parity == 0) & ((x == 1) | (x == 2)))
        def _():
            sent(3)
            sent(4)

        @pl.when((row_parity == 1) & (x == 0))
        def _():
            sent(2)

        @pl.when((x == 3) & (next_parity == 1))
        def _():
            sent(4)

        @pl.when((row_parity == 1) & (x == 3))
        def _():
            sent(5)

        @pl.when((x == 0) & (prev_parity == 1))
        def _():
            sent(3)

    for step in range(4):
        down_copy(step).wait_send()
        sib_copy(step, y, core).wait_send()
    for step in range(3):
        up_copy(step).wait_send()
        sib_copy(4 + step, y, core).wait_send()
    for hop in range(1, NX):
        pick_copy(hop, x).wait_send()
    for copy in out_copies:
        copy.wait()


def on_device(queries, keyvals, seg_len, seg_task, task_slot, prefix_bank):
    anywhere = pl.BlockSpec(memory_space=pl.ANY)
    bf16 = jnp.bfloat16
    return pl.pallas_call(
        kernel,
        out_shape=jax.ShapeDtypeStruct((1, T, H * HD), bf16),
        in_specs=[
            anywhere,
            anywhere,
            anywhere,
            anywhere,
            pl.BlockSpec(memory_space=pltpu.SMEM),
            anywhere,
        ],
        out_specs=anywhere,
        scratch_shapes=[
            pltpu.VMEM((T, H * HD), bf16),
            pltpu.VMEM((KVH, 2, SLOTS, HD), bf16),
            pltpu.VMEM((KVH, 2, T, HD), bf16),
            pltpu.VMEM((NY, 2, ROWS6, PREFIX, KVH * HD), bf16),
            pltpu.VMEM((NX - 1, 2, 2, PREFIX, KVH * HD), bf16),
            pltpu.VMEM((NX, 2, 2, PREFIX, KVH * HD), bf16),
            pltpu.VMEM((KVH, GROUPS, T, 2 * HD), jnp.float32),
            pltpu.VMEM((KVH, GROUPS, T, HD), jnp.float32),
            pltpu.VMEM((T, KEYS), jnp.float32),
            pltpu.VMEM((T, 2 * PREFIX), jnp.float32),
            pltpu.VMEM((T, H * HD), bf16),
            pltpu.VMEM((1, SEGS), jnp.int32),
            pltpu.VMEM((1, SEGS), jnp.int32),
            pltpu.SemaphoreType.DMA((8,)),
            pltpu.SemaphoreType.DMA((KVH,)),
            pltpu.SemaphoreType.DMA((6, KVH)),
            pltpu.SemaphoreType.DMA((4, KVH)),
            pltpu.SemaphoreType.DMA((7,)),
            pltpu.SemaphoreType.DMA((7,)),
            pltpu.SemaphoreType.DMA((7,)),
            pltpu.SemaphoreType.DMA((7,)),
            pltpu.SemaphoreType.DMA((NX - 1,)),
            pltpu.SemaphoreType.DMA((NX - 1,)),
        ],
        compiler_params=pltpu.CompilerParams(
            collective_id=0, has_side_effects=True, vmem_limit_bytes=48 << 20
        ),
    )(queries, keyvals, seg_len, seg_task, task_slot, prefix_bank)


def solution(mesh):
    in_specs = (
        P(None, ("ctx", "grp"), None),
        P(None, None, ("ctx", "grp"), None),
        P(),
        P(),
        P(),
        P(None, "grp", None, None),
    )
    out_specs = P(None, ("ctx", "grp"), None)
    return jax.shard_map(
        on_device, mesh=mesh, in_specs=in_specs, out_specs=out_specs, check_vma=False
    )
```

time: 147 us -> 67.8 us (0.46)
  the two profiles are of different devices: /device:TPU:961 before, /device:TPU:8 now
where the time goes in v1:
time: 67.8 us; the launch traced here: 67.5 us
  Pallas kernels  61.4 us (91%)
  local copies, waits for them, and re-layouts  6.11 us (9%)
    pallas_call x1, Pallas kernels, on_device(): pl.pallas_call(kernel, out_shape=jax.ShapeDtypeStruct((1, T, H * HD), bf1...  61.4 us
    unnamed x13, local copies, waits for them, and re-layouts  6.11 us

profile of v1, /device:TPU:8, one launch (start us, length us, event | category | flops | bytes accessed | tf_op | source)
XLA Modules:
  0.0 67.5 jit_solution(12936491898140332969)
XLA Ops:
  0.0 0.0 copy-start
  0.0 1.2 %copy-done = bf16[1,128,4096]{2,1,0:T(8,128)(2,1)S(1)} copy-done((bf16[1,128,4096]{2,1,0:T(8,128)(2,1)S(1)}, bf16[1,128,4096]{2,1,0:T(8,128)(2,1)}, u32[]{:S(2)}) %copy-start) | copy-done | bytes 1048600
  1.2 0.0 copy-start.1
  1.2 0.9 %copy-done.1 = bf16[2,1,128,512]{3,2,1,0:T(8,128)(2,1)S(1)} copy-done((bf16[2,1,128,512]{3,2,1,0:T(8,128)(2,1)S(1)}, bf16[2,1,128,512]{3,2,1,0:T(8,128)(2,1)}, u32[]{:S(2)}) %copy-start.1) | copy-done | bytes 262168
  2.2 0.0 copy-start.2
  2.2 0.9 %copy-done.2 = bf16[2,6,16,512]{3,2,1,0:T(8,128)(2,1)S(1)} copy-done((bf16[2,6,16,512]{3,2,1,0:T(8,128)(2,1)S(1)}, bf16[2,6,16,512]{3,2,1,0:T(8,128)(2,1)}, u32[]{:S(2)}) %copy-start.2) | copy-done | bytes 196632
  3.1 0.0 copy-start.3
  3.1 0.7 %copy-done.3 = s32[1,512]{1,0:T(1,128)S(1)} copy-done((s32[1,512]{1,0:T(1,128)S(1)}, s32[1,512]{1,0:T(1,128)}, u32[]{:S(2)}) %copy-start.3) | copy-done | bytes 2072
  3.8 0.0 copy-start.4
  3.8 0.7 %copy-done.4 = s32[1,512]{1,0:T(1,128)S(1)} copy-done((s32[1,512]{1,0:T(1,128)S(1)}, s32[1,512]{1,0:T(1,128)}, u32[]{:S(2)}) %copy-start.4) | copy-done | bytes 2072
  4.5 0.0 copy-start.5
  4.5 0.7 %copy-done.5 = s32[192]{0:T(256)S(1)} copy-done((s32[192]{0:T(256)S(1)}, s32[192]{0:T(256)}, u32[]{:S(2)}) %copy-start.5) | copy-done | bytes 792
  5.1 61.4 %shard_map.64 = bf16[1,128,4096]{2,1,0:T(8,128)(2,1)S(1)} custom-call(bf16[1,128,4096]{2,1,0:T(8,128)(2,1)S(1)} %copy-done, bf16[2,1,128,512]{3,2,1,0:T(8,128)(2,1)S(1)} %copy-done.1, s32[1,512]{1,0:T(1,128)S(1)} %copy-done.3, s32[1,512]{1,0:T(1,128)S(1)} %copy-done.4, s32[192]{0:T(256)S(1)} %copy-done.5, bf16[2,6,16,512]{3,2,1,0:T(8,128)(2,1)S(1)} %copy-done.2), custom_call_target="tpu_custom_call" | custom-call | tf_op jit(solution)/shard_map/pallas_call | solution.py:441
  66.5 1.0 %copy.8 = bf16[1,128,4096]{2,1,0:T(8,128)(2,1)} copy(bf16[1,128,4096]{2,1,0:T(8,128)(2,1)S(1)} %shard_map.64) | data formatting | bytes 2097152
Async XLA Ops:
  0.0 1.2 %copy-start = (bf16[1,128,4096]{2,1,0:T(8,128)(2,1)S(1)}, bf16[1,128,4096]{2,1,0:T(8,128)(2,1)}, u32[]{:S(2)}) copy-start(bf16[1,128,4096]{2,1,0:T(8,128)(2,1)} %q_hbm.1) | copy-start | bytes 3145732
  1.2 0.9 %copy-start.1 = (bf16[2,1,128,512]{3,2,1,0:T(8,128)(2,1)S(1)}, bf16[2,1,128,512]{3,2,1,0:T(8,128)(2,1)}, u32[]{:S(2)}) copy-start(bf16[2,1,128,512]{3,2,1,0:T(8,128)(2,1)} %kv_hbm.1) | copy-start | bytes 786436
  2.2 0.9 %copy-start.2 = (bf16[2,6,16,512]{3,2,1,0:T(8,128)(2,1)S(1)}, bf16[2,6,16,512]{3,2,1,0:T(8,128)(2,1)}, u32[]{:S(2)}) copy-start(bf16[2,6,16,512]{3,2,1,0:T(8,128)(2,1)} %bank_hbm.1) | copy-start | bytes 589828
  3.1 0.7 %copy-start.3 = (s32[1,512]{1,0:T(1,128)S(1)}, s32[1,512]{1,0:T(1,128)}, u32[]{:S(2)}) copy-start(s32[1,512]{1,0:T(1,128)} %len_hbm.1) | copy-start | bytes 6148
  3.8 0.7 %copy-start.4 = (s32[1,512]{1,0:T(1,128)S(1)}, s32[1,512]{1,0:T(1,128)}, u32[]{:S(2)}) copy-start(s32[1,512]{1,0:T(1,128)} %task_hbm.1) | copy-start | bytes 6148
  4.5 0.7 %copy-start.5 = (s32[192]{0:T(256)S(1)}, s32[192]{0:T(256)}, u32[]{:S(2)}) copy-start(s32[192]{0:T(256)} %slot_smem.1) | copy-start | bytes 2308

commit v2 on v1

v2 whole, which is shorter than its diff:
```python
import math

import jax
import jax.numpy as jnp
from jax import lax
from jax.experimental import pallas as pl
from jax.experimental.pallas import tpu as pltpu
from jax.sharding import PartitionSpec as P

H = 32
KVH = 4
HD = 128
GROUPS = H // KVH
T = 128
PREFIX = 16
SEGS = 512
ROWS6 = 6
HALF = ROWS6 // 2
NX = 4
NY = 8
KEYS = 4 * T
SLOTS = KEYS + 2 * PREFIX
EXP_SCALE = math.log2(math.e) / math.sqrt(HD)
NEG = -1e30
BIG = 1 << 30


def scan_lanes(row):
    lane = lax.broadcasted_iota(jnp.int32, row.shape, 1)
    step = 1
    while step < row.shape[1]:
        row = row + jnp.where(lane >= step, pltpu.roll(row, step, 1), 0)
        step *= 2
    return row


def kernel(
    q_hbm,
    kv_hbm,
    len_hbm,
    task_hbm,
    slot_smem,
    bank_hbm,
    out_hbm,
    q_buf,
    kv_buf,
    pass_buf,
    col_bank,
    pick_out,
    pick_in,
    acc_buf,
    max_buf,
    bias_buf,
    late_bias_buf,
    out_buf,
    len_buf,
    task_buf,
    local_sem,
    out_sem,
    kv_send,
    kv_recv,
    ring_send,
    ring_recv,
    sib_send,
    sib_recv,
    pick_send,
    pick_recv,
    ready_sem,
):
    ctx = lax.axis_index("ctx")
    grp = lax.axis_index("grp")
    n_ctx = lax.axis_size("ctx")
    core = ctx % 2
    x = grp % NX
    y = grp // NX
    shard = ctx * (NX * NY) + grp

    zero = shard == 0
    live = shard != 0
    twin = (ctx == 1) & (grp == 0)
    late = (ctx == 0) & (y == 0)
    mate = late & (x > 0)
    last = (ctx == n_ctx - 1) & (y == NY - 1)

    next_ctx = jnp.where(y == NY - 1, (ctx + 1) % n_ctx, ctx)
    prev_ctx = jnp.where(y == 0, (ctx + n_ctx - 1) % n_ctx, ctx)
    odd_row = core == 1
    odd_next = next_ctx % 2 == 1
    odd_prev = prev_ctx % 2 == 1
    up = (y + 1) % NY
    down = (y + NY - 1) % NY

    def in_row(col):
        return {"ctx": ctx, "grp": y * NX + col}

    def in_next(col):
        return {"ctx": next_ctx, "grp": up * NX + col}

    def in_prev(col):
        return {"ctx": prev_ctx, "grp": down * NX + col}

    def ring_node(half, row):
        skip = (ctx < 2) & (x == 0) & (row == 0)
        return {"ctx": jnp.where(skip, 1, ctx - core + half), "grp": row * NX + x}

    sibling = {"ctx": ctx + 1 - 2 * core, "grp": grp}
    first_device = {"ctx": 0, "grp": 0}
    twin_device = {"ctx": 1, "grp": 0}

    barrier = pltpu.get_barrier_semaphore()

    def greet(device):
        pl.semaphore_signal(barrier, inc=1, device_id=device, device_id_type=pl.DeviceIdType.MESH)

    row_wise = live & (x > 0) & ((y == 0) | (y == NY - 1))
    corner_down = live & (x == 0)
    corner_up = (x == NX - 1) & ~last

    @pl.when(live)
    def _():
        for hop in range(1, NX):
            col = (x + hop) % NX

            @pl.when(~(late & (col == 0)))
            def _():
                greet(in_row(col))

        greet(ring_node(core, up))
        greet(ring_node(core, down))

        @pl.when(~twin)
        def _():
            greet(sibling)

        @pl.when(mate)
        def _():
            greet(twin_device)
            greet(first_device)

        @pl.when(twin)
        def _():
            greet(ring_node(0, up))
            greet(ring_node(0, down))
            greet(first_device)
            for col in range(1, NX):
                greet({"ctx": 0, "grp": col})

        @pl.when(row_wise & (y == NY - 1))
        def _():
            greet(in_next(x))

        @pl.when(row_wise & (y == 0))
        def _():
            greet(in_prev(x))

        @pl.when(corner_down)
        def _():
            greet(in_prev(NX - 1))

        @pl.when(corner_up)
        def _():
            greet(in_next(0))

    kv_local = []
    bank_local = pltpu.make_async_copy(bank_hbm, col_bank.at[y], local_sem.at[4])
    bank_local.start()
    for j in range(KVH):
        copy = pltpu.make_async_copy(
            kv_hbm.at[:, 0, :, pl.ds(j * HD, HD)],
            kv_buf.at[j, :, pl.ds(0, T), :],
            local_sem.at[j],
        )
        copy.start()
        kv_local.append(copy)
    len_copy = pltpu.make_async_copy(len_hbm, len_buf, local_sem.at[5])
    len_copy.start()
    task_copy = pltpu.make_async_copy(task_hbm, task_buf, local_sem.at[6])
    task_copy.start()
    q_copy = pltpu.make_async_copy(q_hbm.at[0], q_buf, local_sem.at[7])
    q_copy.start()

    def one(flag):
        return jnp.where(flag, 1, 0)

    at_0, at_3 = x == 0, x == NX - 1
    not_0, not_3 = x > 0, x < NX - 1
    inner = ((x == 1) & ~late) | (x == 2)
    back_1 = at_3 & ~late
    pass_on = ~odd_row & inner | (last & (x == 2))
    detour_up = at_3 & odd_next
    relay_3 = at_3 & odd_row
    relay_1 = at_0 & odd_row
    relay_2 = ~odd_row & inner
    detour_down = at_0 & odd_prev
    relay_late = late & (x == 1)

    partners = 6 + 4 * one(twin) + one(row_wise) + one(corner_down) + one(corner_up)
    pl.semaphore_wait(barrier, jnp.where(zero, 4, partners))

    @pl.when(zero)
    def _():
        for device in ([{"ctx": 0, "grp": col} for col in range(1, NX)] + [twin_device]):
            pl.semaphore_signal(
                ready_sem, inc=1, device_id=device, device_id_type=pl.DeviceIdType.MESH
            )

    def slot_ref(j, slot):
        if slot == 4:
            return pass_buf.at[j]
        return kv_buf.at[j, :, pl.ds(slot * T, T), :]

    sends = []

    def kv_copy(j, number, source, device, target):
        return pltpu.make_async_remote_copy(
            src_ref=slot_ref(j, source),
            dst_ref=slot_ref(j, target),
            send_sem=kv_send.at[number, j],
            recv_sem=kv_recv.at[target - 1, j],
            device_id=device,
            device_id_type=pl.DeviceIdType.MESH,
        )

    def send_kv(flag, j, number, source, device, target):
        @pl.when(flag)
        def _():
            kv_copy(j, number, source, device, target).start()

        sends.append((flag, j, number))

    def wait_kv(flag, j, slot):
        @pl.when(flag)
        def _():
            kv_copy(j, 0, slot, sibling, slot).wait_recv()

    def ring_copy(half, number, part, owner, device):
        piece = col_bank.at[owner, part, pl.ds(HALF * half, HALF)]
        return pltpu.make_async_remote_copy(
            src_ref=piece,
            dst_ref=piece,
            send_sem=ring_send.at[half, number, part],
            recv_sem=ring_recv.at[half, number, part],
            device_id=device,
            device_id_type=pl.DeviceIdType.MESH,
        )

    def sib_copy(number, part, owner, half):
        piece = col_bank.at[owner, part, pl.ds(HALF * half, HALF)]
        return pltpu.make_async_remote_copy(
            src_ref=piece,
            dst_ref=piece,
            send_sem=sib_send.at[number, part],
            recv_sem=sib_recv.at[number, part],
            device_id=sibling,
            device_id_type=pl.DeviceIdType.MESH,
        )

    def down_copy(half, step, part):
        return ring_copy(half, step, part, (y + step) % NY, ring_node(half, down))

    def up_copy(half, step, part):
        return ring_copy(half, 4 + step, part, (y + NY - step) % NY, ring_node(half, up))

    bank_local.wait()

    @pl.when(live)
    def _():
        for part in range(2):
            down_copy(core, 0, part).start()
            up_copy(core, 0, part).start()

    @pl.when(twin)
    def _():
        for part in range(2):
            down_copy(0, 0, part).start()
            up_copy(0, 0, part).start()

    for j in range(KVH):
        kv_local[j].wait()
        send_kv(not_3, j, 0, 0, in_row((x + 1) % NX), 1)
        send_kv(not_0, j, 1, 0, in_next(x), 4)
        send_kv(at_0, j, 1, 0, in_row(NX - 1), 3)

    len_copy.wait()
    task_copy.wait()
    lengths = len_buf[...]
    starts = scan_lanes(lengths) - lengths
    tasks = task_buf[...]

    def segments(first):
        start_a = jnp.max(jnp.where(starts <= first, starts, 0))
        start_b = jnp.min(jnp.where(starts > first, starts, BIG))
        return start_a, start_b

    def bank_row(start):
        task = jnp.sum(jnp.where(starts == start, tasks, 0))
        row = slot_smem[task]
        owner = (row * 10923) >> 16
        return owner % NX, owner // NX, row - ROWS6 * owner

    slot_a = jnp.where(late & (x == 1), 2, 1)
    slot_b = jnp.where(late & (x == 3), 2, 3)
    slot_late = jnp.where(late & (x == 1), 1, jnp.where(late & (x == 3), 3, 2))

    here_a, here_b = segments(shard * T)
    rel_a = here_a - shard * T
    rel_b = here_b - shard * T

    query_at = lax.broadcasted_iota(jnp.int32, (T, T), 0)
    column = lax.broadcasted_iota(jnp.int32, (T, T), 1)
    earliest = jnp.where(query_at < rel_b, rel_a, rel_b)

    def block_bias(slot):
        key_at = column - slot * T
        return jnp.where((key_at >= earliest) & (key_at <= query_at), 0.0, NEG)

    bias_buf[:, pl.ds(0, T)] = block_bias(0)
    bias_buf[:, pl.ds(T, T)] = block_bias(slot_a)
    bias_buf[:, pl.ds(2 * T, T)] = block_bias(slot_b)
    late_bias_buf[:, pl.ds(0, T)] = block_bias(slot_late)
    query_at = lax.broadcasted_iota(jnp.int32, (T, 2 * PREFIX), 0)
    column_p = lax.broadcasted_iota(jnp.int32, (T, 2 * PREFIX), 1)
    late_bias_buf[:, pl.ds(T, 2 * PREFIX)] = jnp.where(
        (query_at < rel_b) == (column_p < PREFIX), 0.0, NEG
    )

    def wanted(first):
        return [bank_row(start) for start in segments(first)]

    row_wants = [wanted((shard - x + (x + hop) % NX) * T) for hop in range(NX)]

    q_copy.wait()

    def row_keys(j, blocks):
        keys = jnp.concatenate(
            [kv_buf[j, 0, pl.ds(pl.multiple_of(s * T, T), T), :] for s in blocks], axis=0
        )
        values = jnp.concatenate(
            [kv_buf[j, 1, pl.ds(pl.multiple_of(s * T, T), T), :] for s in blocks], axis=0
        )
        count = len(blocks) * T
        values = jnp.concatenate([values, jnp.ones((count, HD), jnp.bfloat16)], axis=1)
        for g in range(GROUPS):
            query = q_buf[:, pl.ds(pl.multiple_of((j * GROUPS + g) * HD, HD), HD)]
            scores = lax.dot_general(
                query, keys, (((1,), (1,)), ((), ())), preferred_element_type=jnp.float32
            )
            scores = scores + bias_buf[:, pl.ds(0, count)]
            top = jnp.max(scores, axis=1, keepdims=True)
            weights = jnp.exp2((scores - top) * EXP_SCALE).astype(jnp.bfloat16)
            acc_buf[j, g] = jnp.dot(weights, values, preferred_element_type=jnp.float32)
            max_buf[j, g] = jnp.broadcast_to(top, (T, HD))

    def first_level(j):
        wait_kv(x > 0, j, 4)
        send_kv(inner, j, 2, 4, in_row((x + 3) % NX), 3)
        send_kv(at_3, j, 2, 4, in_row(2), 3)
        send_kv(back_1, j, 3, 4, in_row(0), 1)
        wait_kv((x > 1) | ((x == 1) & ~late), j, 1)
        send_kv(pass_on, j, 3, 1, in_row((x + 1) % NX), 2)
        send_kv(detour_up, j, 4, 1, in_next(0), 2)
        wait_kv((x == 3) & ~late, j, 3)
        send_kv(relay_3, j, 5, 3, in_row(2), 2)

    def second_level(j):
        wait_kv(x == 0, j, 1)
        send_kv(relay_1, j, 2, 1, in_row(1), 2)
        wait_kv(x < 3, j, 3)
        send_kv(relay_2, j, 4, 3, in_row((x + 3) % NX), 2)
        send_kv(detour_down, j, 3, 3, in_prev(NX - 1), 2)
        wait_kv(late & (x != 2), j, 2)
        row_keys(j, (0, slot_a, slot_b))

    def ring_step(half, step, share):
        for part in range(2):
            ring_copy(half, step, part, (y + 1 + step) % NY, sibling).wait_recv()
            if step < 3:
                down_copy(half, step + 1, part).start()
            if share is not None:

                @pl.when(share)
                def _():
                    sib_copy(step, part, (y + 1 + step) % NY, half).start()

            if step < 3:
                owner = (y + NY - 1 - step) % NY
                ring_copy(half, 4 + step, part, owner, sibling).wait_recv()
                if step < 2:
                    up_copy(half, step + 1, part).start()
                if share is not None:

                    @pl.when(share)
                    def _():
                        sib_copy(4 + step, part, owner, half).start()

    def both_rings(step):
        ring_step(core, step, ~twin)

        @pl.when(twin)
        def _():
            ring_step(0, step, None)

    ring_owners = [(step, (y + 1 + step) % NY) for step in range(4)]
    ring_owners += [(4 + step, (y + NY - 1 - step) % NY) for step in range(3)]

    def pick_copy(number, slot, device):
        return pltpu.make_async_remote_copy(
            src_ref=pick_out.at[number],
            dst_ref=pick_in.at[slot],
            send_sem=pick_send.at[number],
            recv_sem=pick_recv.at[slot],
            device_id=device,
            device_id_type=pl.DeviceIdType.MESH,
        )

    def pick(ref, place, wants):
        for which in range(2):
            _, owner_y, row = wants[which]
            ref[place, which] = col_bank[owner_y, :, row]

    @pl.when(live)
    def _():
        both_rings(0)
        first_level(0)
        first_level(1)
        both_rings(1)
        first_level(2)
        second_level(0)
        first_level(3)
        both_rings(2)
        second_level(1)
        second_level(2)
        both_rings(3)
        second_level(3)

        @pl.when(~twin)
        def _():
            for number, owner in ring_owners:
                for part in range(2):
                    sib_copy(number, part, owner, 1 - core).wait_recv()

        for hop in (2, 1, 3):
            col = (x + hop) % NX

            @pl.when(~(late & (col == 0)))
            def _():
                pick(pick_out, hop - 1, row_wants[hop])
                pick_copy(hop - 1, hop, in_row(col)).start()

        pick(pick_in, 0, row_wants[0])

        @pl.when(twin)
        def _():
            for col in range(NX):
                pick(pick_out, NX - 1 + col, wanted(col * T))
            for col in range(1, NX):
                pick_copy(NX - 1 + col, col, {"ctx": 0, "grp": col}).start()
            pl.semaphore_wait(ready_sem, 1)
            pick_copy(NX - 1, 0, first_device).start()

        @pl.when(mate)
        def _():
            pl.semaphore_wait(ready_sem, 1)
            for hop in range(1, NX):

                @pl.when((x + hop) % NX == 0)
                def _():
                    pick(pick_out, hop - 1, row_wants[hop])
                    pick_copy(hop - 1, hop, first_device).start()

    @pl.when(zero)
    def _():
        for j in range(KVH):
            kv_buf[j, :, pl.ds(2 * T, T), :] = jnp.zeros((2, T, HD), jnp.bfloat16)
            row_keys(j, (0,))
        pick_copy(0, 0, twin_device).wait_recv()

    for hop in range(1, NX):
        pick_copy(0, hop, sibling).wait_recv()
    for which in range(2):
        owner_x, _, _ = row_wants[0][which]
        row = pick_in[(x + NX - owner_x) % NX, which]
        for j in range(KVH):
            for part in range(2):
                kv_buf[j, part, pl.ds(KEYS + which * PREFIX, PREFIX), :] = row[
                    part, :, j * HD : (j + 1) * HD
                ]

    out_copies = []
    for j in range(KVH):

        @pl.when(live)
        def _():
            pltpu.make_async_remote_copy(
                src_ref=kv_buf.at[j, :, pl.ds(0, T), :],
                dst_ref=kv_buf.at[j, :, pl.ds(slot_late * T, T), :],
                send_sem=kv_send.at[0, j],
                recv_sem=kv_recv.at[slot_late - 1, j],
                device_id=sibling,
                device_id_type=pl.DeviceIdType.MESH,
            ).wait_recv()

        send_kv(relay_late, j, 3, 1, in_row(2), 2)
        due = pl.ds(pl.multiple_of(slot_late * T, T), T)
        prefix = pl.ds(KEYS, 2 * PREFIX)
        keys = jnp.concatenate([kv_buf[j, 0, due, :], kv_buf[j, 0, prefix, :]], axis=0)
        values = jnp.concatenate([kv_buf[j, 1, due, :], kv_buf[j, 1, prefix, :]], axis=0)
        values = jnp.concatenate(
            [values, jnp.ones((T + 2 * PREFIX, HD), jnp.bfloat16)], axis=1
        )
        for g in range(GROUPS):
            query = q_buf[:, pl.ds((j * GROUPS + g) * HD, HD)]
            scores = lax.dot_general(
                query, keys, (((1,), (1,)), ((), ())), preferred_element_type=jnp.float32
            )
            scores = scores + late_bias_buf[...]
            old_top = max_buf[j, g]
            top = jnp.maximum(old_top, jnp.max(scores, axis=1, keepdims=True))
            shrink = jnp.exp2((old_top - top) * EXP_SCALE)
            tops = jnp.concatenate([top, top[:, : 2 * PREFIX]], axis=1)
            weights = jnp.exp2((scores - tops) * EXP_SCALE).astype(jnp.bfloat16)
            fresh = jnp.dot(weights, values, preferred_element_type=jnp.float32)
            mixed = acc_buf[j, g, :, pl.ds(0, HD)] * shrink + fresh[:, :HD]
            total = acc_buf[j, g, :, pl.ds(HD, HD)] * shrink + fresh[:, HD:]
            out_buf[:, pl.ds((j * GROUPS + g) * HD, HD)] = (mixed / total).astype(jnp.bfloat16)
        span = pl.ds(j * GROUPS * HD, GROUPS * HD)
        copy = pltpu.make_async_copy(out_buf.at[:, span], out_hbm.at[0, :, span], out_sem.at[j])
        copy.start()
        out_copies.append(copy)

    for flag, j, number in sends:
        own = number < 2
        keep = flag if own else flag & live

        @pl.when(keep)
        def _():
            kv_copy(j, number, 0, sibling, 1).wait_send()

    @pl.when(live)
    def _():
        for part in range(2):
            for step in range(4):
                down_copy(core, step, part).wait_send()
            for step in range(3):
                up_copy(core, step, part).wait_send()
        for hop in range(1, NX):
            pick_copy(hop - 1, hop, sibling).wait_send()

        @pl.when(~twin)
        def _():
            for number, owner in ring_owners:
                for part in range(2):
                    sib_copy(number, part, owner, core).wait_send()

        @pl.when(twin)
        def _():
            for part in range(2):
                for step in range(4):
                    down_copy(0, step, part).wait_send()
                for step in range(3):
                    up_copy(0, step, part).wait_send()
            for col in range(NX):
                pick_copy(NX - 1 + col, col, first_device).wait_send()

    for copy in out_copies:
        copy.wait()


def on_device(queries, keyvals, seg_len, seg_task, task_slot, prefix_bank):
    anywhere = pl.BlockSpec(memory_space=pl.ANY)
    bf16 = jnp.bfloat16
    return pl.pallas_call(
        kernel,
        out_shape=jax.ShapeDtypeStruct((1, T, H * HD), bf16),
        in_specs=[
            anywhere,
            anywhere,
            anywhere,
            anywhere,
            pl.BlockSpec(memory_space=pltpu.SMEM),
            anywhere,
        ],
        out_specs=anywhere,
        scratch_shapes=[
            pltpu.VMEM((T, H * HD), bf16),
            pltpu.VMEM((KVH, 2, SLOTS, HD), bf16),
            pltpu.VMEM((KVH, 2, T, HD), bf16),
            pltpu.VMEM((NY, 2, ROWS6, PREFIX, KVH * HD), bf16),
            pltpu.VMEM((2 * NX - 1, 2, 2, PREFIX, KVH * HD), bf16),
            pltpu.VMEM((NX, 2, 2, PREFIX, KVH * HD), bf16),
            pltpu.VMEM((KVH, GROUPS, T, 2 * HD), jnp.float32),
            pltpu.VMEM((KVH, GROUPS, T, HD), jnp.float32),
            pltpu.VMEM((T, KEYS - T), jnp.float32),
            pltpu.VMEM((T, T + 2 * PREFIX), jnp.float32),
            pltpu.VMEM((T, H * HD), bf16),
            pltpu.VMEM((1, SEGS), jnp.int32),
            pltpu.VMEM((1, SEGS), jnp.int32),
            pltpu.SemaphoreType.DMA((8,)),
            pltpu.SemaphoreType.DMA((KVH,)),
            pltpu.SemaphoreType.DMA((6, KVH)),
            pltpu.SemaphoreType.DMA((4, KVH)),
            pltpu.SemaphoreType.DMA((2, 7, 2)),
            pltpu.SemaphoreType.DMA((2, 7, 2)),
            pltpu.SemaphoreType.DMA((7, 2)),
            pltpu.SemaphoreType.DMA((7, 2)),
            pltpu.SemaphoreType.DMA((2 * NX - 1,)),
            pltpu.SemaphoreType.DMA((NX,)),
            pltpu.SemaphoreType.REGULAR,
        ],
        compiler_params=pltpu.CompilerParams(
            collective_id=0, has_side_effects=True, vmem_limit_bytes=67043328
        ),
    )(queries, keyvals, seg_len, seg_task, task_slot, prefix_bank)


def solution(mesh):
    in_specs = (
        P(None, ("ctx", "grp"), None),
        P(None, None, ("ctx", "grp"), None),
        P(),
        P(),
        P(),
        P(None, "grp", None, None),
    )
    out_specs = P(None, ("ctx", "grp"), None)
    return jax.shard_map(
        on_device, mesh=mesh, in_specs=in_specs, out_specs=out_specs, check_vma=False
    )
```

time: 67.8 us -> 55.8 us (0.82)
  the two profiles are of different devices: /device:TPU:8 before, /device:TPU:4 now
where the time goes in v2:
time: 55.8 us; the launch traced here: 55.6 us
  Pallas kernels  53.3 us (96%)
  local copies, waits for them, and re-layouts  2.29 us (4%)
    pallas_call x1, Pallas kernels, on_device(): pl.pallas_call(kernel, out_shape=jax.ShapeDtypeStruct((1, T, H * HD), bf1...  53.3 us
    unnamed x1, local copies, waits for them, and re-layouts  2.29 us

profile of v2, /device:TPU:4, one launch (start us, length us, event | category | flops | bytes accessed | tf_op | source)
XLA Modules:
  0.0 55.6 jit_solution(11925156267752937702)
XLA Ops:
  0.0 53.3 %shard_map.64 = bf16[1,128,4096]{2,1,0:T(8,128)(2,1)} custom-call(bf16[1,128,4096]{2,1,0:T(8,128)(2,1)} %q_hbm.1, bf16[2,1,128,512]{3,2,1,0:T(8,128)(2,1)} %kv_hbm.1, s32[1,512]{1,0:T(1,128)} %len_hbm.1, s32[1,512]{1,0:T(1,128)} %task_hbm.1, s32[192]{0:T(256)} %slot_smem.1, bf16[2,6,16,512]{3,2,1,0:T(8,128)(2,1)} %bank_hbm.1), custom_call_target="tpu_custom_call" | custom-call | tf_op jit(solution)/shard_map/pallas_call | solution.py:572
  53.3 2.3 %copy.8 = bf16[1,128,4096]{2,1,0:T(8,128)(2,1)} copy(bf16[1,128,4096]{2,1,0:T(8,128)(2,1)} %shard_map.64) | data formatting | bytes 2097152

commit v3 on v2

--- a/solution.py
+++ b/solution.py
@@ -112,7 +112,8 @@
     def greet(device):
         pl.semaphore_signal(barrier, inc=1, device_id=device, device_id_type=pl.DeviceIdType.MESH)
 
-    row_wise = live & (x > 0) & ((y == 0) | (y == NY - 1))
+    wrap_up = (x > 0) & (y == NY - 1) & ~last
+    wrap_down = (x > 0) & (y == 0) & ~late
     corner_down = live & (x == 0)
     corner_up = (x == NX - 1) & ~last
 
@@ -145,11 +146,11 @@
             for col in range(1, NX):
                 greet({"ctx": 0, "grp": col})
 
-        @pl.when(row_wise & (y == NY - 1))
+        @pl.when(wrap_up)
         def _():
             greet(in_next(x))
 
-        @pl.when(row_wise & (y == 0))
+        @pl.when(wrap_down)
         def _():
             greet(in_prev(x))
 
@@ -183,10 +184,12 @@
         return jnp.where(flag, 1, 0)
 
     at_0, at_3 = x == 0, x == NX - 1
-    not_0, not_3 = x > 0, x < NX - 1
-    inner = ((x == 1) & ~late) | (x == 2)
-    back_1 = at_3 & ~late
-    pass_on = ~odd_row & inner | (last & (x == 2))
+    not_3 = x < NX - 1
+    give_up = (x > 0) & ~last
+    take_up = (x > 0) & ~late
+    inner = ((x == 1) | (x == 2)) & ~late
+    back = at_3 & ~late
+    pass_on = ~odd_row & (((x == 1) & ~late) | (x == 2)) | (last & (x == 2))
     detour_up = at_3 & odd_next
     relay_3 = at_3 & odd_row
     relay_1 = at_0 & odd_row
@@ -194,7 +197,7 @@
     detour_down = at_0 & odd_prev
     relay_late = late & (x == 1)
 
-    partners = 6 + 4 * one(twin) + one(row_wise) + one(corner_down) + one(corner_up)
+    partners = 6 + 4 * one(twin) + one(wrap_up | wrap_down) + one(corner_down) + one(corner_up)
     pl.semaphore_wait(barrier, jnp.where(zero, 4, partners))
 
     @pl.when(zero)
@@ -234,7 +237,7 @@
             kv_copy(j, 0, slot, sibling, slot).wait_recv()
 
     def ring_copy(half, number, part, owner, device):
-        piece = col_bank.at[owner, part, pl.ds(HALF * half, HALF)]
+        piece = col_bank.at[owner, :, HALF * half + part]
         return pltpu.make_async_remote_copy(
             src_ref=piece,
             dst_ref=piece,
@@ -245,7 +248,7 @@
         )
 
     def sib_copy(number, part, owner, half):
-        piece = col_bank.at[owner, part, pl.ds(HALF * half, HALF)]
+        piece = col_bank.at[owner, :, HALF * half + part]
         return pltpu.make_async_remote_copy(
             src_ref=piece,
             dst_ref=piece,
@@ -265,21 +268,113 @@
 
     @pl.when(live)
     def _():
-        for part in range(2):
+        for part in range(HALF):
             down_copy(core, 0, part).start()
+
+    @pl.when(twin)
+    def _():
+        for part in range(HALF):
+            down_copy(0, 0, part).start()
+
+    def give(j):
+        send_kv(give_up, j, 1, 0, in_next(x), 4)
+
+    kv_local[0].wait()
+    give(0)
+
+    @pl.when(live)
+    def _():
+        for part in range(HALF):
             up_copy(core, 0, part).start()
 
     @pl.when(twin)
     def _():
-        for part in range(2):
-            down_copy(0, 0, part).start()
+        for part in range(HALF):
             up_copy(0, 0, part).start()
 
     for j in range(KVH):
-        kv_local[j].wait()
+        if j > 0:
+            kv_local[j].wait()
         send_kv(not_3, j, 0, 0, in_row((x + 1) % NX), 1)
-        send_kv(not_0, j, 1, 0, in_next(x), 4)
         send_kv(at_0, j, 1, 0, in_row(NX - 1), 3)
+    give(1)
+
+    def first_level(j):
+        wait_kv(take_up, j, 4)
+        send_kv(inner, j, 2, 4, in_row((x + 3) % NX), 3)
+        send_kv(back, j, 2, 4, in_row(2), 3)
+        send_kv(back, j, 3, 4, in_row(0), 1)
+        wait_kv((x > 1) | ((x == 1) & ~late), j, 1)
+        send_kv(pass_on, j, 3, 1, in_row((x + 1) % NX), 2)
+        send_kv(detour_up, j, 4, 1, in_next(0), 2)
+        wait_kv((x == 3) & ~late, j, 3)
+        send_kv(relay_3, j, 5, 3, in_row(2), 2)
+
+    def second_level(j):
+        wait_kv(x == 0, j, 1)
+        send_kv(relay_1, j, 2, 1, in_row(1), 2)
+        wait_kv((x < 3) & ~late, j, 3)
+        send_kv(relay_2, j, 4, 3, in_row((x + 3) % NX), 2)
+        send_kv(detour_down, j, 3, 3, in_prev(NX - 1), 2)
+        wait_kv(late & at_3, j, 2)
+
+    def ring_step(half, step, share):
+        for part in range(HALF):
+            ring_copy(half, step, part, (y + 1 + step) % NY, sibling).wait_recv()
+            if step < 3:
+                down_copy(half, step + 1, part).start()
+            if share is not None:
+
+                @pl.when(share)
+                def _():
+                    sib_copy(step, part, (y + 1 + step) % NY, half).start()
+
+            if step < 3:
+                owner = (y + NY - 1 - step) % NY
+                ring_copy(half, 4 + step, part, owner, sibling).wait_recv()
+                if step < 2:
+                    up_copy(half, step + 1, part).start()
+                if share is not None:
+
+                    @pl.when(share)
+                    def _():
+                        sib_copy(4 + step, part, owner, half).start()
+
+    def both_rings(step):
+        ring_step(core, step, ~twin)
+
+        @pl.when(twin)
+        def _():
+            ring_step(0, step, None)
+
+    ring_owners = [(step, (y + 1 + step) % NY) for step in range(4)]
+    ring_owners += [(4 + step, (y + NY - 1 - step) % NY) for step in range(3)]
+
+    def pick_copy(number, slot, device):
+        return pltpu.make_async_remote_copy(
+            src_ref=pick_out.at[number],
+            dst_ref=pick_in.at[slot],
+            send_sem=pick_send.at[number],
+            recv_sem=pick_recv.at[slot],
+            device_id=device,
+            device_id_type=pl.DeviceIdType.MESH,
+        )
+
+    def pick(ref, place, wants):
+        for which in range(2):
+            _, owner_y, row = wants[which]
+            ref[place, which] = col_bank[owner_y, :, row]
+
+    @pl.when(live)
+    def _():
+        both_rings(0)
+
+    give(2)
+
+    @pl.when(live)
+    def _():
+        first_level(0)
+        first_level(1)
 
     len_copy.wait()
     task_copy.wait()
@@ -317,6 +412,7 @@
     bias_buf[:, pl.ds(0, T)] = block_bias(0)
     bias_buf[:, pl.ds(T, T)] = block_bias(slot_a)
     bias_buf[:, pl.ds(2 * T, T)] = block_bias(slot_b)
+    bias_buf[:, pl.ds(3 * T, T)] = block_bias(slot_late)
     late_bias_buf[:, pl.ds(0, T)] = block_bias(slot_late)
     query_at = lax.broadcasted_iota(jnp.int32, (T, 2 * PREFIX), 0)
     column_p = lax.broadcasted_iota(jnp.int32, (T, 2 * PREFIX), 1)
@@ -327,7 +423,71 @@
     def wanted(first):
         return [bank_row(start) for start in segments(first)]
 
+
+    @pl.when(live)
+    def _():
+        both_rings(1)
+
+    give(3)
+
+    @pl.when(live)
+    def _():
+        second_level(0)
+        first_level(2)
+
     row_wants = [wanted((shard - x + (x + hop) % NX) * T) for hop in range(NX)]
+
+    for slot in (2, 3):
+
+        @pl.when(late & (x < slot))
+        def _():
+            for j in range(KVH):
+                kv_buf[j, :, pl.ds(slot * T, T), :] = jnp.zeros((2, T, HD), jnp.bfloat16)
+
+    @pl.when(live)
+    def _():
+        both_rings(2)
+        second_level(1)
+        first_level(3)
+        second_level(2)
+        both_rings(3)
+
+        @pl.when(~twin)
+        def _():
+            for number, owner in ring_owners:
+                for part in range(HALF):
+                    sib_copy(number, part, owner, 1 - core).wait_recv()
+
+        for hop in (2, 1, 3):
+            col = (x + hop) % NX
+
+            @pl.when(~(late & (col == 0)))
+            def _():
+                pick(pick_out, hop - 1, row_wants[hop])
+                pick_copy(hop - 1, hop, in_row(col)).start()
+
+        pick(pick_in, 0, row_wants[0])
+
+        second_level(3)
+
+        @pl.when(twin)
+        def _():
+            for col in range(NX):
+                pick(pick_out, NX - 1 + col, wanted(col * T))
+            for col in range(1, NX):
+                pick_copy(NX - 1 + col, col, {"ctx": 0, "grp": col}).start()
+            pl.semaphore_wait(ready_sem, 1)
+            pick_copy(NX - 1, 0, first_device).start()
+
+        @pl.when(mate)
+        def _():
+            pl.semaphore_wait(ready_sem, 1)
+            for hop in range(1, NX):
+
+                @pl.when((x + hop) % NX == 0)
+                def _():
+                    pick(pick_out, hop - 1, row_wants[hop])
+                    pick_copy(hop - 1, hop, first_device).start()
 
     q_copy.wait()
 
@@ -351,128 +511,26 @@
             acc_buf[j, g] = jnp.dot(weights, values, preferred_element_type=jnp.float32)
             max_buf[j, g] = jnp.broadcast_to(top, (T, HD))
 
-    def first_level(j):
-        wait_kv(x > 0, j, 4)
-        send_kv(inner, j, 2, 4, in_row((x + 3) % NX), 3)
-        send_kv(at_3, j, 2, 4, in_row(2), 3)
-        send_kv(back_1, j, 3, 4, in_row(0), 1)
-        wait_kv((x > 1) | ((x == 1) & ~late), j, 1)
-        send_kv(pass_on, j, 3, 1, in_row((x + 1) % NX), 2)
-        send_kv(detour_up, j, 4, 1, in_next(0), 2)
-        wait_kv((x == 3) & ~late, j, 3)
-        send_kv(relay_3, j, 5, 3, in_row(2), 2)
-
-    def second_level(j):
-        wait_kv(x == 0, j, 1)
-        send_kv(relay_1, j, 2, 1, in_row(1), 2)
-        wait_kv(x < 3, j, 3)
-        send_kv(relay_2, j, 4, 3, in_row((x + 3) % NX), 2)
-        send_kv(detour_down, j, 3, 3, in_prev(NX - 1), 2)
-        wait_kv(late & (x != 2), j, 2)
-        row_keys(j, (0, slot_a, slot_b))
-
-    def ring_step(half, step, share):
-        for part in range(2):
-            ring_copy(half, step, part, (y + 1 + step) % NY, sibling).wait_recv()
-            if step < 3:
-                down_copy(half, step + 1, part).start()
-            if share is not None:
-
-                @pl.when(share)
-                def _():
-                    sib_copy(step, part, (y + 1 + step) % NY, half).start()
-
-            if step < 3:
-                owner = (y + NY - 1 - step) % NY
-                ring_copy(half, 4 + step, part, owner, sibling).wait_recv()
-                if step < 2:
-                    up_copy(half, step + 1, part).start()
-                if share is not None:
-
-                    @pl.when(share)
-                    def _():
-                        sib_copy(4 + step, part, owner, half).start()
-
-    def both_rings(step):
-        ring_step(core, step, ~twin)
-
-        @pl.when(twin)
-        def _():
-            ring_step(0, step, None)
-
-    ring_owners = [(step, (y + 1 + step) % NY) for step in range(4)]
-    ring_owners += [(4 + step, (y + NY - 1 - step) % NY) for step in range(3)]
-
-    def pick_copy(number, slot, device):
-        return pltpu.make_async_remote_copy(
-            src_ref=pick_out.at[number],
-            dst_ref=pick_in.at[slot],
-            send_sem=pick_send.at[number],
-            recv_sem=pick_recv.at[slot],
-            device_id=device,
-            device_id_type=pl.DeviceIdType.MESH,
-        )
-
-    def pick(ref, place, wants):
-        for which in range(2):
-            _, owner_y, row = wants[which]
-            ref[place, which] = col_bank[owner_y, :, row]
-
-    @pl.when(live)
-    def _():
-        both_rings(0)
-        first_level(0)
-        first_level(1)
-        both_rings(1)
-        first_level(2)
-        second_level(0)
-        first_level(3)
-        both_rings(2)
-        second_level(1)
-        second_level(2)
-        both_rings(3)
-        second_level(3)
-
-        @pl.when(~twin)
-        def _():
-            for number, owner in ring_owners:
-                for part in range(2):
-                    sib_copy(number, part, owner, 1 - core).wait_recv()
-
-        for hop in (2, 1, 3):
-            col = (x + hop) % NX
-
-            @pl.when(~(late & (col == 0)))
-            def _():
-                pick(pick_out, hop - 1, row_wants[hop])
-                pick_copy(hop - 1, hop, in_row(col)).start()
-
-        pick(pick_in, 0, row_wants[0])
-
-        @pl.when(twin)
-        def _():
-            for col in range(NX):
-                pick(pick_out, NX - 1 + col, wanted(col * T))
-            for col in range(1, NX):
-                pick_copy(NX - 1 + col, col, {"ctx": 0, "grp": col}).start()
-            pl.semaphore_wait(ready_sem, 1)
-            pick_copy(NX - 1, 0, first_device).start()
-
-        @pl.when(mate)
-        def _():
-            pl.semaphore_wait(ready_sem, 1)
-            for hop in range(1, NX):
-
-                @pl.when((x + hop) % NX == 0)
-                def _():
-                    pick(pick_out, hop - 1, row_wants[hop])
-                    pick_copy(hop - 1, hop, first_device).start()
+    normal = ~late
+
+    @pl.when(normal)
+    def _():
+        for j in range(KVH):
+            wait_kv(normal, j, 2)
+            row_keys(j, (0, 1, 3, 2))
+
+    @pl.when(mate)
+    def _():
+        @pl.loop(0, KVH)
+        def _(j):
+            row_keys(j, (0, slot_a, slot_b))
 
     @pl.when(zero)
     def _():
-        for j in range(KVH):
-            kv_buf[j, :, pl.ds(2 * T, T), :] = jnp.zeros((2, T, HD), jnp.bfloat16)
+        @pl.loop(0, KVH)
+        def _(j):
             row_keys(j, (0,))
+
         pick_copy(0, 0, twin_device).wait_recv()
 
     for hop in range(1, NX):
@@ -486,47 +544,65 @@
                     part, :, j * HD : (j + 1) * HD
                 ]
 
-    out_copies = []
-    for j in range(KVH):
-
-        @pl.when(live)
-        def _():
-            pltpu.make_async_remote_copy(
-                src_ref=kv_buf.at[j, :, pl.ds(0, T), :],
-                dst_ref=kv_buf.at[j, :, pl.ds(slot_late * T, T), :],
-                send_sem=kv_send.at[0, j],
-                recv_sem=kv_recv.at[slot_late - 1, j],
-                device_id=sibling,
-                device_id_type=pl.DeviceIdType.MESH,
-            ).wait_recv()
-
-        send_kv(relay_late, j, 3, 1, in_row(2), 2)
-        due = pl.ds(pl.multiple_of(slot_late * T, T), T)
+    def finish(j, due):
         prefix = pl.ds(KEYS, 2 * PREFIX)
-        keys = jnp.concatenate([kv_buf[j, 0, due, :], kv_buf[j, 0, prefix, :]], axis=0)
-        values = jnp.concatenate([kv_buf[j, 1, due, :], kv_buf[j, 1, prefix, :]], axis=0)
-        values = jnp.concatenate(
-            [values, jnp.ones((T + 2 * PREFIX, HD), jnp.bfloat16)], axis=1
-        )
+        keys = kv_buf[j, 0, prefix, :]
+        values = kv_buf[j, 1, prefix, :]
+        bias = late_bias_buf[:, pl.ds(T, 2 * PREFIX)]
+        if due:
+            block = pl.ds(pl.multiple_of(slot_late * T, T), T)
+            keys = jnp.concatenate([kv_buf[j, 0, block, :], keys], axis=0)
+            values = jnp.concatenate([kv_buf[j, 1, block, :], values], axis=0)
+            bias = late_bias_buf[...]
+        count = values.shape[0]
+        values = jnp.concatenate([values, jnp.ones((count, HD), jnp.bfloat16)], axis=1)
         for g in range(GROUPS):
-            query = q_buf[:, pl.ds((j * GROUPS + g) * HD, HD)]
+            head = pl.ds(pl.multiple_of((j * GROUPS + g) * HD, HD), HD)
             scores = lax.dot_general(
-                query, keys, (((1,), (1,)), ((), ())), preferred_element_type=jnp.float32
+                q_buf[:, head], keys, (((1,), (1,)), ((), ())), preferred_element_type=jnp.float32
             )
-            scores = scores + late_bias_buf[...]
+            scores = scores + bias
             old_top = max_buf[j, g]
             top = jnp.maximum(old_top, jnp.max(scores, axis=1, keepdims=True))
             shrink = jnp.exp2((old_top - top) * EXP_SCALE)
-            tops = jnp.concatenate([top, top[:, : 2 * PREFIX]], axis=1)
+            tops = top[:, : 2 * PREFIX]
+            if due:
+                tops = jnp.concatenate([top, tops], axis=1)
             weights = jnp.exp2((scores - tops) * EXP_SCALE).astype(jnp.bfloat16)
             fresh = jnp.dot(weights, values, preferred_element_type=jnp.float32)
             mixed = acc_buf[j, g, :, pl.ds(0, HD)] * shrink + fresh[:, :HD]
             total = acc_buf[j, g, :, pl.ds(HD, HD)] * shrink + fresh[:, HD:]
-            out_buf[:, pl.ds((j * GROUPS + g) * HD, HD)] = (mixed / total).astype(jnp.bfloat16)
-        span = pl.ds(j * GROUPS * HD, GROUPS * HD)
-        copy = pltpu.make_async_copy(out_buf.at[:, span], out_hbm.at[0, :, span], out_sem.at[j])
-        copy.start()
-        out_copies.append(copy)
+            out_buf[:, head] = (mixed / total).astype(jnp.bfloat16)
+        span = pl.ds(pl.multiple_of(j * GROUPS * HD, GROUPS * HD), GROUPS * HD)
+        pltpu.make_async_copy(out_buf.at[:, span], out_hbm.at[0, :, span], out_sem.at[j]).start()
+
+    @pl.when(normal)
+    def _():
+        for j in range(KVH):
+            finish(j, False)
+
+    @pl.when(late)
+    def _():
+        @pl.loop(0, KVH)
+        def _(j):
+            @pl.when(mate)
+            def _():
+                pltpu.make_async_remote_copy(
+                    src_ref=kv_buf.at[j, :, pl.ds(0, T), :],
+                    dst_ref=kv_buf.at[j, :, pl.ds(slot_late * T, T), :],
+                    send_sem=kv_send.at[0, j],
+                    recv_sem=kv_recv.at[slot_late - 1, j],
+                    device_id=sibling,
+                    device_id_type=pl.DeviceIdType.MESH,
+                ).wait_recv()
+
+            @pl.when(relay_late)
+            def _():
+                kv_copy(j, 3, 1, in_row(2), 2).start()
+
+            finish(j, True)
+
+    sends.extend((relay_late, j, 3) for j in range(KVH))
 
     for flag, j, number in sends:
         own = number < 2
@@ -538,7 +614,7 @@
 
     @pl.when(live)
     def _():
-        for part in range(2):
+        for part in range(HALF):
             for step in range(4):
                 down_copy(core, step, part).wait_send()
             for step in range(3):
@@ -549,12 +625,12 @@
         @pl.when(~twin)
         def _():
             for number, owner in ring_owners:
-                for part in range(2):
+                for part in range(HALF):
                     sib_copy(number, part, owner, core).wait_send()
 
         @pl.when(twin)
         def _():
-            for part in range(2):
+            for part in range(HALF):
                 for step in range(4):
                     down_copy(0, step, part).wait_send()
                 for step in range(3):
@@ -562,8 +638,9 @@
             for col in range(NX):
                 pick_copy(NX - 1 + col, col, first_device).wait_send()
 
-    for copy in out_copies:
-        copy.wait()
+    for j in range(KVH):
+        span = pl.ds(j * GROUPS * HD, GROUPS * HD)
+        pltpu.make_async_copy(out_buf.at[:, span], out_hbm.at[0, :, span], out_sem.at[j]).wait()
 
 
 def on_device(queries, keyvals, seg_len, seg_task, task_slot, prefix_bank):
@@ -590,7 +667,7 @@
             pltpu.VMEM((NX, 2, 2, PREFIX, KVH * HD), bf16),
             pltpu.VMEM((KVH, GROUPS, T, 2 * HD), jnp.float32),
             pltpu.VMEM((KVH, GROUPS, T, HD), jnp.float32),
-            pltpu.VMEM((T, KEYS - T), jnp.float32),
+            pltpu.VMEM((T, KEYS), jnp.float32),
             pltpu.VMEM((T, T + 2 * PREFIX), jnp.float32),
             pltpu.VMEM((T, H * HD), bf16),
             pltpu.VMEM((1, SEGS), jnp.int32),
@@ -599,10 +676,10 @@
             pltpu.SemaphoreType.DMA((KVH,)),
             pltpu.SemaphoreType.DMA((6, KVH)),
             pltpu.SemaphoreType.DMA((4, KVH)),
-            pltpu.SemaphoreType.DMA((2, 7, 2)),
-            pltpu.SemaphoreType.DMA((2, 7, 2)),
-            pltpu.SemaphoreType.DMA((7, 2)),
-            pltpu.SemaphoreType.DMA((7, 2)),
+            pltpu.SemaphoreType.DMA((2, 7, HALF)),
+            pltpu.SemaphoreType.DMA((2, 7, HALF)),
+            pltpu.SemaphoreType.DMA((7, HALF)),
+            pltpu.SemaphoreType.DMA((7, HALF)),
             pltpu.SemaphoreType.DMA((2 * NX - 1,)),
             pltpu.SemaphoreType.DMA((NX,)),
             pltpu.SemaphoreType.REGULAR,

time: 55.8 us -> 41.7 us (0.75)
  Pallas kernels: 53.3 us -> 39 us
    pallas_call x1, Pallas kernels: 53.3 us -> 39 us  [on_device(): pl.pallas_call(kernel, out_shape=jax.ShapeDtypeStruct((1, T, H * HD), bf1...]
where the time goes in v3:
time: 41.7 us; the launch traced here: 41.3 us
  Pallas kernels  39 us (94%)
  local copies, waits for them, and re-layouts  2.29 us (5%)
    pallas_call x1, Pallas kernels, on_device(): pl.pallas_call(kernel, out_shape=jax.ShapeDtypeStruct((1, T, H * HD), bf1...  39 us
    unnamed x1, local copies, waits for them, and re-layouts  2.29 us

profile of v3, /device:TPU:4, one launch (start us, length us, event | category | flops | bytes accessed | tf_op | source)
XLA Modules:
  0.0 41.3 jit_solution(18330900691658938457)
XLA Ops:
  0.0 39.0 %shard_map.64 = bf16[1,128,4096]{2,1,0:T(8,128)(2,1)} custom-call(bf16[1,128,4096]{2,1,0:T(8,128)(2,1)} %q_hbm.1, bf16[2,1,128,512]{3,2,1,0:T(8,128)(2,1)} %kv_hbm.1, s32[1,512]{1,0:T(1,128)} %len_hbm.1, s32[1,512]{1,0:T(1,128)} %task_hbm.1, s32[192]{0:T(256)} %slot_smem.1, bf16[2,6,16,512]{3,2,1,0:T(8,128)(2,1)} %bank_hbm.1), custom_call_target="tpu_custom_call" | custom-call | tf_op jit(solution)/shard_map/pallas_call | solution.py:649
  39.0 2.3 %copy.8 = bf16[1,128,4096]{2,1,0:T(8,128)(2,1)} copy(bf16[1,128,4096]{2,1,0:T(8,128)(2,1)} %shard_map.64) | data formatting | bytes 2097152

commit v4 on v3

--- a/solution.py
+++ b/solution.py
@@ -63,6 +63,8 @@
     ring_recv,
     sib_send,
     sib_recv,
+    cross_send,
+    cross_recv,
     pick_send,
     pick_recv,
     ready_sem,
@@ -84,9 +86,7 @@
 
     next_ctx = jnp.where(y == NY - 1, (ctx + 1) % n_ctx, ctx)
     prev_ctx = jnp.where(y == 0, (ctx + n_ctx - 1) % n_ctx, ctx)
-    odd_row = core == 1
-    odd_next = next_ctx % 2 == 1
-    odd_prev = prev_ctx % 2 == 1
+    pair = (ctx // 2) % 2
     up = (y + 1) % NY
     down = (y + NY - 1) % NY
 
@@ -103,6 +103,10 @@
         skip = (ctx < 2) & (x == 0) & (row == 0)
         return {"ctx": jnp.where(skip, 1, ctx - core + half), "grp": row * NX + x}
 
+    def cross_node(half):
+        far = ctx - core + half + 2 - 4 * pair
+        return {"ctx": jnp.where((far == 0) & (grp == 0), 1, far), "grp": grp}
+
     sibling = {"ctx": ctx + 1 - 2 * core, "grp": grp}
     first_device = {"ctx": 0, "grp": 0}
     twin_device = {"ctx": 1, "grp": 0}
@@ -114,8 +118,6 @@
 
     wrap_up = (x > 0) & (y == NY - 1) & ~last
     wrap_down = (x > 0) & (y == 0) & ~late
-    corner_down = live & (x == 0)
-    corner_up = (x == NX - 1) & ~last
 
     @pl.when(live)
     def _():
@@ -128,6 +130,7 @@
 
         greet(ring_node(core, up))
         greet(ring_node(core, down))
+        greet(cross_node(core))
 
         @pl.when(~twin)
         def _():
@@ -142,6 +145,7 @@
         def _():
             greet(ring_node(0, up))
             greet(ring_node(0, down))
+            greet(cross_node(0))
             greet(first_device)
             for col in range(1, NX):
                 greet({"ctx": 0, "grp": col})
@@ -153,14 +157,6 @@
         @pl.when(wrap_down)
         def _():
             greet(in_prev(x))
-
-        @pl.when(corner_down)
-        def _():
-            greet(in_prev(NX - 1))
-
-        @pl.when(corner_up)
-        def _():
-            greet(in_next(0))
 
     kv_local = []
     bank_local = pltpu.make_async_copy(bank_hbm, col_bank.at[y], local_sem.at[4])
@@ -183,21 +179,13 @@
     def one(flag):
         return jnp.where(flag, 1, 0)
 
-    at_0, at_3 = x == 0, x == NX - 1
-    not_3 = x < NX - 1
     give_up = (x > 0) & ~last
     take_up = (x > 0) & ~late
-    inner = ((x == 1) | (x == 2)) & ~late
-    back = at_3 & ~late
-    pass_on = ~odd_row & (((x == 1) & ~late) | (x == 2)) | (last & (x == 2))
-    detour_up = at_3 & odd_next
-    relay_3 = at_3 & odd_row
-    relay_1 = at_0 & odd_row
-    relay_2 = ~odd_row & inner
-    detour_down = at_0 & odd_prev
-    relay_late = late & (x == 1)
-
-    partners = 6 + 4 * one(twin) + one(wrap_up | wrap_down) + one(corner_down) + one(corner_up)
+    reaches = [x + hop < NX for hop in range(1, NX)]
+    spreads = [take_up & (x >= hop) for hop in range(1, NX)]
+    from_1, from_2 = x >= 2, x == 3
+
+    partners = 7 + 5 * one(twin) + one(wrap_up | wrap_down)
     pl.semaphore_wait(barrier, jnp.where(zero, 4, partners))
 
     @pl.when(zero)
@@ -236,116 +224,106 @@
         def _():
             kv_copy(j, 0, slot, sibling, slot).wait_recv()
 
-    def ring_copy(half, number, part, owner, device):
-        piece = col_bank.at[owner, :, HALF * half + part]
+    def piece(owner, part, half):
+        return col_bank.at[owner, part, pl.ds(HALF * half, HALF)]
+
+    def bank_copy(ref, send_sem, recv_sem, device):
         return pltpu.make_async_remote_copy(
-            src_ref=piece,
-            dst_ref=piece,
-            send_sem=ring_send.at[half, number, part],
-            recv_sem=ring_recv.at[half, number, part],
+            src_ref=ref,
+            dst_ref=ref,
+            send_sem=send_sem,
+            recv_sem=recv_sem,
             device_id=device,
             device_id_type=pl.DeviceIdType.MESH,
         )
 
-    def sib_copy(number, part, owner, half):
-        piece = col_bank.at[owner, :, HALF * half + part]
-        return pltpu.make_async_remote_copy(
-            src_ref=piece,
-            dst_ref=piece,
-            send_sem=sib_send.at[number, part],
-            recv_sem=sib_recv.at[number, part],
-            device_id=sibling,
-            device_id_type=pl.DeviceIdType.MESH,
-        )
-
-    def down_copy(half, step, part):
-        return ring_copy(half, step, part, (y + step) % NY, ring_node(half, down))
-
-    def up_copy(half, step, part):
-        return ring_copy(half, 4 + step, part, (y + NY - step) % NY, ring_node(half, up))
+    def ring_copy(half, number, owner, device):
+        ref = piece(owner, pair, half)
+        return bank_copy(ref, ring_send.at[half, number], ring_recv.at[half, number], device)
+
+    def cross_copy(half, number, owner, part):
+        ref = piece(owner, part, half)
+        sems = (cross_send.at[half, number], cross_recv.at[half, number])
+        return bank_copy(ref, *sems, cross_node(half))
+
+    def sib_copy(turn, number, owner, half):
+        ref = piece(owner, pair if turn == 0 else 1 - pair, half)
+        return bank_copy(ref, sib_send.at[turn, number], sib_recv.at[turn, number], sibling)
+
+    def down_copy(half, step):
+        return ring_copy(half, step, (y + step) % NY, ring_node(half, down))
+
+    def up_copy(half, step):
+        return ring_copy(half, 4 + step, (y + NY - step) % NY, ring_node(half, up))
 
     bank_local.wait()
 
     @pl.when(live)
     def _():
-        for part in range(HALF):
-            down_copy(core, 0, part).start()
+        down_copy(core, 0).start()
 
     @pl.when(twin)
     def _():
-        for part in range(HALF):
-            down_copy(0, 0, part).start()
+        down_copy(0, 0).start()
 
     def give(j):
-        send_kv(give_up, j, 1, 0, in_next(x), 4)
+        send_kv(give_up, j, 3, 0, in_next(x), 4)
 
     kv_local[0].wait()
     give(0)
 
     @pl.when(live)
     def _():
-        for part in range(HALF):
-            up_copy(core, 0, part).start()
+        up_copy(core, 0).start()
 
     @pl.when(twin)
     def _():
-        for part in range(HALF):
-            up_copy(0, 0, part).start()
+        up_copy(0, 0).start()
 
     for j in range(KVH):
         if j > 0:
             kv_local[j].wait()
-        send_kv(not_3, j, 0, 0, in_row((x + 1) % NX), 1)
-        send_kv(at_0, j, 1, 0, in_row(NX - 1), 3)
+        for hop in range(1, NX):
+            send_kv(reaches[hop - 1], j, hop - 1, 0, in_row((x + hop) % NX), hop)
     give(1)
 
-    def first_level(j):
+    def spread(j):
         wait_kv(take_up, j, 4)
-        send_kv(inner, j, 2, 4, in_row((x + 3) % NX), 3)
-        send_kv(back, j, 2, 4, in_row(2), 3)
-        send_kv(back, j, 3, 4, in_row(0), 1)
-        wait_kv((x > 1) | ((x == 1) & ~late), j, 1)
-        send_kv(pass_on, j, 3, 1, in_row((x + 1) % NX), 2)
-        send_kv(detour_up, j, 4, 1, in_next(0), 2)
-        wait_kv((x == 3) & ~late, j, 3)
-        send_kv(relay_3, j, 5, 3, in_row(2), 2)
-
-    def second_level(j):
-        wait_kv(x == 0, j, 1)
-        send_kv(relay_1, j, 2, 1, in_row(1), 2)
-        wait_kv((x < 3) & ~late, j, 3)
-        send_kv(relay_2, j, 4, 3, in_row((x + 3) % NX), 2)
-        send_kv(detour_down, j, 3, 3, in_prev(NX - 1), 2)
-        wait_kv(late & at_3, j, 2)
+        for hop in (2, 1, 3):
+            send_kv(spreads[hop - 1], j, 3 + hop, 4, in_row((x + NX - hop) % NX), NX - hop)
 
     def ring_step(half, step, share):
-        for part in range(HALF):
-            ring_copy(half, step, part, (y + 1 + step) % NY, sibling).wait_recv()
-            if step < 3:
-                down_copy(half, step + 1, part).start()
-            if share is not None:
-
-                @pl.when(share)
-                def _():
-                    sib_copy(step, part, (y + 1 + step) % NY, half).start()
-
-            if step < 3:
-                owner = (y + NY - 1 - step) % NY
-                ring_copy(half, 4 + step, part, owner, sibling).wait_recv()
-                if step < 2:
-                    up_copy(half, step + 1, part).start()
-                if share is not None:
-
-                    @pl.when(share)
-                    def _():
-                        sib_copy(4 + step, part, owner, half).start()
-
-    def both_rings(step):
-        ring_step(core, step, ~twin)
+        arrivals = [(step, (y + 1 + step) % NY)]
+        if step < 3:
+            arrivals.append((4 + step, (y + NY - 1 - step) % NY))
+        for number, owner in arrivals:
+            ring_copy(half, number, owner, sibling).wait_recv()
+            if number < 3:
+                down_copy(half, step + 1).start()
+            if 4 <= number < 6:
+                up_copy(half, step + 1).start()
+            cross_copy(half, number, owner, pair).start()
+            if share:
+                sib_copy(0, number, owner, half).start()
+
+    def cross_step(half, step, share):
+        arrivals = [(step, (y + 1 + step) % NY)]
+        if step < 3:
+            arrivals.append((4 + step, (y + NY - 1 - step) % NY))
+        for number, owner in arrivals:
+            cross_copy(half, number, owner, 1 - pair).wait_recv()
+            if share:
+                sib_copy(1, number, owner, half).start()
+
+    def on_rings(stage, step):
+        @pl.when(~twin)
+        def _():
+            stage(core, step, True)
 
         @pl.when(twin)
         def _():
-            ring_step(0, step, None)
+            stage(1, step, False)
+            stage(0, step, False)
 
     ring_owners = [(step, (y + 1 + step) % NY) for step in range(4)]
     ring_owners += [(4 + step, (y + NY - 1 - step) % NY) for step in range(3)]
@@ -367,14 +345,13 @@
 
     @pl.when(live)
     def _():
-        both_rings(0)
+        on_rings(ring_step, 0)
 
     give(2)
 
     @pl.when(live)
     def _():
-        first_level(0)
-        first_level(1)
+        spread(0)
 
     len_copy.wait()
     task_copy.wait()
@@ -426,14 +403,14 @@
 
     @pl.when(live)
     def _():
-        both_rings(1)
+        on_rings(ring_step, 1)
 
     give(3)
 
     @pl.when(live)
     def _():
-        second_level(0)
-        first_level(2)
+        on_rings(cross_step, 0)
+        spread(1)
 
     row_wants = [wanted((shard - x + (x + hop) % NX) * T) for hop in range(NX)]
 
@@ -446,17 +423,19 @@
 
     @pl.when(live)
     def _():
-        both_rings(2)
-        second_level(1)
-        first_level(3)
-        second_level(2)
-        both_rings(3)
+        on_rings(ring_step, 2)
+        on_rings(cross_step, 1)
+        spread(2)
+        on_rings(ring_step, 3)
+        on_rings(cross_step, 2)
+        spread(3)
+        on_rings(cross_step, 3)
 
         @pl.when(~twin)
         def _():
             for number, owner in ring_owners:
-                for part in range(HALF):
-                    sib_copy(number, part, owner, 1 - core).wait_recv()
+                for turn in range(2):
+                    sib_copy(turn, number, owner, 1 - core).wait_recv()
 
         for hop in (2, 1, 3):
             col = (x + hop) % NX
@@ -467,8 +446,6 @@
                 pick_copy(hop - 1, hop, in_row(col)).start()
 
         pick(pick_in, 0, row_wants[0])
-
-        second_level(3)
 
         @pl.when(twin)
         def _():
@@ -516,13 +493,16 @@
     @pl.when(normal)
     def _():
         for j in range(KVH):
-            wait_kv(normal, j, 2)
+            for slot in (1, 3, 2):
+                wait_kv(normal, j, slot)
             row_keys(j, (0, 1, 3, 2))
 
     @pl.when(mate)
     def _():
         @pl.loop(0, KVH)
         def _(j):
+            wait_kv(from_1, j, 1)
+            wait_kv(from_2, j, 2)
             row_keys(j, (0, slot_a, slot_b))
 
     @pl.when(zero)
@@ -596,17 +576,10 @@
                     device_id_type=pl.DeviceIdType.MESH,
                 ).wait_recv()
 
-            @pl.when(relay_late)
-            def _():
-                kv_copy(j, 3, 1, in_row(2), 2).start()
-
             finish(j, True)
 
-    sends.extend((relay_late, j, 3) for j in range(KVH))
-
     for flag, j, number in sends:
-        own = number < 2
-        keep = flag if own else flag & live
+        keep = flag if number < 4 else flag & live
 
         @pl.when(keep)
         def _():
@@ -614,27 +587,29 @@
 
     @pl.when(live)
     def _():
-        for part in range(HALF):
-            for step in range(4):
-                down_copy(core, step, part).wait_send()
-            for step in range(3):
-                up_copy(core, step, part).wait_send()
+        for step in range(4):
+            down_copy(core, step).wait_send()
+        for step in range(3):
+            up_copy(core, step).wait_send()
+        for number, owner in ring_owners:
+            cross_copy(core, number, owner, pair).wait_send()
         for hop in range(1, NX):
             pick_copy(hop - 1, hop, sibling).wait_send()
 
         @pl.when(~twin)
         def _():
             for number, owner in ring_owners:
-                for part in range(HALF):
-                    sib_copy(number, part, owner, core).wait_send()
+                for turn in range(2):
+                    sib_copy(turn, number, owner, core).wait_send()
 
         @pl.when(twin)
         def _():
-            for part in range(HALF):
-                for step in range(4):
-                    down_copy(0, step, part).wait_send()
-                for step in range(3):
-                    up_copy(0, step, part).wait_send()
+            for step in range(4):
+                down_copy(0, step).wait_send()
+            for step in range(3):
+                up_copy(0, step).wait_send()
+            for number, owner in ring_owners:
+                cross_copy(0, number, owner, pair).wait_send()
             for col in range(NX):
                 pick_copy(NX - 1 + col, col, first_device).wait_send()
 
@@ -674,12 +649,14 @@
             pltpu.VMEM((1, SEGS), jnp.int32),
             pltpu.SemaphoreType.DMA((8,)),
             pltpu.SemaphoreType.DMA((KVH,)),
-            pltpu.SemaphoreType.DMA((6, KVH)),
+            pltpu.SemaphoreType.DMA((7, KVH)),
             pltpu.SemaphoreType.DMA((4, KVH)),
-            pltpu.SemaphoreType.DMA((2, 7, HALF)),
-            pltpu.SemaphoreType.DMA((2, 7, HALF)),
-            pltpu.SemaphoreType.DMA((7, HALF)),
-            pltpu.SemaphoreType.DMA((7, HALF)),
+            pltpu.SemaphoreType.DMA((2, 7)),
+            pltpu.SemaphoreType.DMA((2, 7)),
+            pltpu.SemaphoreType.DMA((2, 7)),
+            pltpu.SemaphoreType.DMA((2, 7)),
+            pltpu.SemaphoreType.DMA((2, 7)),
+            pltpu.SemaphoreType.DMA((2, 7)),
             pltpu.SemaphoreType.DMA((2 * NX - 1,)),
             pltpu.SemaphoreType.DMA((NX,)),
             pltpu.SemaphoreType.REGULAR,

time: 41.7 us -> 40.7 us (0.976)
  Pallas kernels: 39 us -> 38.1 us
    pallas_call x1, Pallas kernels: 39 us -> 38.1 us  [on_device(): pl.pallas_call(kernel, out_shape=jax.ShapeDtypeStruct((1, T, H * HD), bf1...]
where the time goes in v4:
time: 40.7 us; the launch traced here: 40.4 us
  Pallas kernels  38.1 us (94%)
  local copies, waits for them, and re-layouts  2.29 us (6%)
    pallas_call x1, Pallas kernels, on_device(): pl.pallas_call(kernel, out_shape=jax.ShapeDtypeStruct((1, T, H * HD), bf1...  38.1 us
    unnamed x1, local copies, waits for them, and re-layouts  2.29 us

profile of v4, /device:TPU:4, one launch (start us, length us, event | category | flops | bytes accessed | tf_op | source)
XLA Modules:
  0.0 40.4 jit_solution(6345492555874710729)
XLA Ops:
  0.0 38.1 %shard_map.64 = bf16[1,128,4096]{2,1,0:T(8,128)(2,1)} custom-call(bf16[1,128,4096]{2,1,0:T(8,128)(2,1)} %q_hbm.1, bf16[2,1,128,512]{3,2,1,0:T(8,128)(2,1)} %kv_hbm.1, s32[1,512]{1,0:T(1,128)} %len_hbm.1, s32[1,512]{1,0:T(1,128)} %task_hbm.1, s32[192]{0:T(256)} %slot_smem.1, bf16[2,6,16,512]{3,2,1,0:T(8,128)(2,1)} %bank_hbm.1), custom_call_target="tpu_custom_call" | custom-call | tf_op jit(solution)/shard_map/pallas_call | solution.py:624
  38.2 2.3 %copy.8 = bf16[1,128,4096]{2,1,0:T(8,128)(2,1)} copy(bf16[1,128,4096]{2,1,0:T(8,128)(2,1)} %shard_map.64) | data formatting | bytes 2097152

commit v5 on v4

--- a/solution.py
+++ b/solution.py
@@ -15,7 +15,6 @@
 PREFIX = 16
 SEGS = 512
 ROWS6 = 6
-HALF = ROWS6 // 2
 NX = 4
 NY = 8
 KEYS = 4 * T
@@ -61,10 +60,6 @@
     kv_recv,
     ring_send,
     ring_recv,
-    sib_send,
-    sib_recv,
-    cross_send,
-    cross_recv,
     pick_send,
     pick_recv,
     ready_sem,
@@ -86,7 +81,9 @@
 
     next_ctx = jnp.where(y == NY - 1, (ctx + 1) % n_ctx, ctx)
     prev_ctx = jnp.where(y == 0, (ctx + n_ctx - 1) % n_ctx, ctx)
-    pair = (ctx // 2) % 2
+    other = ctx + 1 - 2 * core
+    pair_ctx = (ctx, other)
+    first_chips = (ctx < 2) & (y == 0)
     up = (y + 1) % NY
     down = (y + NY - 1) % NY
 
@@ -103,10 +100,6 @@
         skip = (ctx < 2) & (x == 0) & (row == 0)
         return {"ctx": jnp.where(skip, 1, ctx - core + half), "grp": row * NX + x}
 
-    def cross_node(half):
-        far = ctx - core + half + 2 - 4 * pair
-        return {"ctx": jnp.where((far == 0) & (grp == 0), 1, far), "grp": grp}
-
     sibling = {"ctx": ctx + 1 - 2 * core, "grp": grp}
     first_device = {"ctx": 0, "grp": 0}
     twin_device = {"ctx": 1, "grp": 0}
@@ -123,32 +116,27 @@
     def _():
         for hop in range(1, NX):
             col = (x + hop) % NX
-
-            @pl.when(~(late & (col == 0)))
-            def _():
-                greet(in_row(col))
+            for target in pair_ctx:
+
+                @pl.when(~(first_chips & (target == 0) & (col == 0)))
+                def _():
+                    greet({"ctx": target, "grp": y * NX + col})
 
         greet(ring_node(core, up))
         greet(ring_node(core, down))
-        greet(cross_node(core))
 
         @pl.when(~twin)
         def _():
             greet(sibling)
 
-        @pl.when(mate)
-        def _():
-            greet(twin_device)
+        @pl.when(first_chips)
+        def _():
             greet(first_device)
 
         @pl.when(twin)
         def _():
             greet(ring_node(0, up))
             greet(ring_node(0, down))
-            greet(cross_node(0))
-            greet(first_device)
-            for col in range(1, NX):
-                greet({"ctx": 0, "grp": col})
 
         @pl.when(wrap_up)
         def _():
@@ -185,12 +173,13 @@
     spreads = [take_up & (x >= hop) for hop in range(1, NX)]
     from_1, from_2 = x >= 2, x == 3
 
-    partners = 7 + 5 * one(twin) + one(wrap_up | wrap_down)
-    pl.semaphore_wait(barrier, jnp.where(zero, 4, partners))
+    partners = 9 - one(first_chips) + 2 * one(twin) + one(wrap_up | wrap_down)
+    pl.semaphore_wait(barrier, jnp.where(zero, 7, partners))
 
     @pl.when(zero)
     def _():
-        for device in ([{"ctx": 0, "grp": col} for col in range(1, NX)] + [twin_device]):
+        devices = [{"ctx": c, "grp": col} for c in range(2) for col in range(NX) if c + col]
+        for device in devices:
             pl.semaphore_signal(
                 ready_sem, inc=1, device_id=device, device_id_type=pl.DeviceIdType.MESH
             )
@@ -224,47 +213,36 @@
         def _():
             kv_copy(j, 0, slot, sibling, slot).wait_recv()
 
-    def piece(owner, part, half):
-        return col_bank.at[owner, part, pl.ds(HALF * half, HALF)]
-
-    def bank_copy(ref, send_sem, recv_sem, device):
+    def ring_copy(part, number, third, owner, device):
+        piece = col_bank.at[owner, part, pl.ds(2 * third, 2)]
         return pltpu.make_async_remote_copy(
-            src_ref=ref,
-            dst_ref=ref,
-            send_sem=send_sem,
-            recv_sem=recv_sem,
+            src_ref=piece,
+            dst_ref=piece,
+            send_sem=ring_send.at[part, number, third],
+            recv_sem=ring_recv.at[part, number, third],
             device_id=device,
             device_id_type=pl.DeviceIdType.MESH,
         )
 
-    def ring_copy(half, number, owner, device):
-        ref = piece(owner, pair, half)
-        return bank_copy(ref, ring_send.at[half, number], ring_recv.at[half, number], device)
-
-    def cross_copy(half, number, owner, part):
-        ref = piece(owner, part, half)
-        sems = (cross_send.at[half, number], cross_recv.at[half, number])
-        return bank_copy(ref, *sems, cross_node(half))
-
-    def sib_copy(turn, number, owner, half):
-        ref = piece(owner, pair if turn == 0 else 1 - pair, half)
-        return bank_copy(ref, sib_send.at[turn, number], sib_recv.at[turn, number], sibling)
-
-    def down_copy(half, step):
-        return ring_copy(half, step, (y + step) % NY, ring_node(half, down))
-
-    def up_copy(half, step):
-        return ring_copy(half, 4 + step, (y + NY - step) % NY, ring_node(half, up))
+    def down_copy(part, step, third):
+        return ring_copy(part, step, third, (y + step) % NY, ring_node(part, down))
+
+    def up_copy(part, step, third):
+        return ring_copy(part, 4 + step, third, (y + NY - step) % NY, ring_node(part, up))
+
+    def first_pieces(part, send):
+        for third in range(3):
+            send(part, 0, third).start()
 
     bank_local.wait()
 
     @pl.when(live)
     def _():
-        down_copy(core, 0).start()
+        first_pieces(core, down_copy)
 
     @pl.when(twin)
     def _():
-        down_copy(0, 0).start()
+        first_pieces(0, down_copy)
 
     def give(j):
         send_kv(give_up, j, 3, 0, in_next(x), 4)
@@ -274,11 +252,11 @@
 
     @pl.when(live)
     def _():
-        up_copy(core, 0).start()
+        first_pieces(core, up_copy)
 
     @pl.when(twin)
     def _():
-        up_copy(0, 0).start()
+        first_pieces(0, up_copy)
 
     for j in range(KVH):
         if j > 0:
@@ -292,60 +270,47 @@
         for hop in (2, 1, 3):
             send_kv(spreads[hop - 1], j, 3 + hop, 4, in_row((x + NX - hop) % NX), NX - hop)
 
-    def ring_step(half, step, share):
-        arrivals = [(step, (y + 1 + step) % NY)]
-        if step < 3:
-            arrivals.append((4 + step, (y + NY - 1 - step) % NY))
-        for number, owner in arrivals:
-            ring_copy(half, number, owner, sibling).wait_recv()
-            if number < 3:
-                down_copy(half, step + 1).start()
-            if 4 <= number < 6:
-                up_copy(half, step + 1).start()
-            cross_copy(half, number, owner, pair).start()
-            if share:
-                sib_copy(0, number, owner, half).start()
-
-    def cross_step(half, step, share):
-        arrivals = [(step, (y + 1 + step) % NY)]
-        if step < 3:
-            arrivals.append((4 + step, (y + NY - 1 - step) % NY))
-        for number, owner in arrivals:
-            cross_copy(half, number, owner, 1 - pair).wait_recv()
-            if share:
-                sib_copy(1, number, owner, half).start()
-
-    def on_rings(stage, step):
-        @pl.when(~twin)
-        def _():
-            stage(core, step, True)
+    def ring_step(part, step):
+        for third in range(3):
+            owner = (y + 1 + step) % NY
+            ring_copy(part, step, third, owner, sibling).wait_recv()
+            if step < 3:
+                down_copy(part, step + 1, third).start()
+                owner = (y + NY - 1 - step) % NY
+                ring_copy(part, 4 + step, third, owner, sibling).wait_recv()
+            if step < 2:
+                up_copy(part, step + 1, third).start()
+
+    def rings(step):
+        ring_step(core, step)
 
         @pl.when(twin)
         def _():
-            stage(1, step, False)
-            stage(0, step, False)
-
-    ring_owners = [(step, (y + 1 + step) % NY) for step in range(4)]
-    ring_owners += [(4 + step, (y + NY - 1 - step) % NY) for step in range(3)]
-
-    def pick_copy(number, slot, device):
+            ring_step(0, step)
+
+    def pick(ref, part, wants):
+        for which in range(2):
+            _, owner_y, row = wants[which]
+            ref[which] = col_bank[owner_y, part, row]
+
+    def pick_copy(group, part, pair, hop, device):
         return pltpu.make_async_remote_copy(
-            src_ref=pick_out.at[number],
-            dst_ref=pick_in.at[slot],
-            send_sem=pick_send.at[number],
-            recv_sem=pick_recv.at[slot],
+            src_ref=pick_out.at[group, pair, hop],
+            dst_ref=pick_in.at[part, hop],
+            send_sem=pick_send.at[group, pair, hop],
+            recv_sem=pick_recv.at[part, hop],
             device_id=device,
             device_id_type=pl.DeviceIdType.MESH,
         )
 
-    def pick(ref, place, wants):
-        for which in range(2):
-            _, owner_y, row = wants[which]
-            ref[place, which] = col_bank[owner_y, :, row]
-
-    @pl.when(live)
-    def _():
-        on_rings(ring_step, 0)
+    def send_pick(group, part, pair, hop):
+        device = {"ctx": pair_ctx[pair], "grp": y * NX + (x + hop) % NX}
+        pick(pick_out.at[group, pair, hop], part, row_wants[pair][hop])
+        pick_copy(group, part, pair, hop, device).start()
+
+    @pl.when(live)
+    def _():
+        rings(0)
 
     give(2)
 
@@ -403,16 +368,18 @@
 
     @pl.when(live)
     def _():
-        on_rings(ring_step, 1)
+        rings(1)
 
     give(3)
 
     @pl.when(live)
     def _():
-        on_rings(cross_step, 0)
         spread(1)
 
-    row_wants = [wanted((shard - x + (x + hop) % NX) * T) for hop in range(NX)]
+    row_wants = [
+        [wanted((c * NX * NY + y * NX + (x + hop) % NX) * T) for hop in range(NX)]
+        for c in pair_ctx
+    ]
 
     for slot in (2, 3):
 
@@ -423,48 +390,47 @@
 
     @pl.when(live)
     def _():
-        on_rings(ring_step, 2)
-        on_rings(cross_step, 1)
+        rings(2)
         spread(2)
-        on_rings(ring_step, 3)
-        on_rings(cross_step, 2)
+        rings(3)
         spread(3)
-        on_rings(cross_step, 3)
+
+        for hop in (2, 1, 3):
+            for pair in range(2):
+                from_first = first_chips & (pair_ctx[pair] == 0) & ((x + hop) % NX == 0)
+
+                @pl.when(~from_first)
+                def _():
+                    send_pick(0, core, pair, hop)
 
         @pl.when(~twin)
         def _():
-            for number, owner in ring_owners:
-                for turn in range(2):
-                    sib_copy(turn, number, owner, 1 - core).wait_recv()
-
-        for hop in (2, 1, 3):
-            col = (x + hop) % NX
-
-            @pl.when(~(late & (col == 0)))
+            send_pick(0, core, 1, 0)
+
+        pick(pick_in.at[core, 0], core, row_wants[0][0])
+
+        @pl.when(twin)
+        def _():
+            for hop in (2, 1, 3):
+                for pair in range(2):
+                    send_pick(1, 0, pair, hop)
+            pick(pick_in.at[0, 0], 0, row_wants[0][0])
+
+        @pl.when(first_chips)
+        def _():
+            pl.semaphore_wait(ready_sem, 1)
+            for hop in range(NX):
+                for pair in range(2):
+                    if pair + hop:
+                        to_first = (pair_ctx[pair] == 0) & ((x + hop) % NX == 0)
+
+                        @pl.when(to_first)
+                        def _():
+                            send_pick(0, core, pair, hop)
+
+            @pl.when(twin)
             def _():
-                pick(pick_out, hop - 1, row_wants[hop])
-                pick_copy(hop - 1, hop, in_row(col)).start()
-
-        pick(pick_in, 0, row_wants[0])
-
-        @pl.when(twin)
-        def _():
-            for col in range(NX):
-                pick(pick_out, NX - 1 + col, wanted(col * T))
-            for col in range(1, NX):
-                pick_copy(NX - 1 + col, col, {"ctx": 0, "grp": col}).start()
-            pl.semaphore_wait(ready_sem, 1)
-            pick_copy(NX - 1, 0, first_device).start()
-
-        @pl.when(mate)
-        def _():
-            pl.semaphore_wait(ready_sem, 1)
-            for hop in range(1, NX):
-
-                @pl.when((x + hop) % NX == 0)
-                def _():
-                    pick(pick_out, hop - 1, row_wants[hop])
-                    pick_copy(hop - 1, hop, first_device).start()
+                send_pick(1, 0, 1, 0)
 
     q_copy.wait()
 
@@ -511,17 +477,22 @@
         def _(j):
             row_keys(j, (0,))
 
-        pick_copy(0, 0, twin_device).wait_recv()
-
-    for hop in range(1, NX):
-        pick_copy(0, hop, sibling).wait_recv()
+        pick_copy(0, 0, 0, 0, twin_device).wait_recv()
+
+    @pl.when(~twin)
+    def _():
+        pick_copy(0, 1 - core, 0, 0, sibling).wait_recv()
+
+    for part in range(2):
+        for hop in range(1, NX):
+            pick_copy(0, part, 0, hop, sibling).wait_recv()
     for which in range(2):
-        owner_x, _, _ = row_wants[0][which]
-        row = pick_in[(x + NX - owner_x) % NX, which]
-        for j in range(KVH):
-            for part in range(2):
+        owner_x, _, _ = row_wants[0][0][which]
+        for part in range(2):
+            row = pick_in[part, (x + NX - owner_x) % NX, which]
+            for j in range(KVH):
                 kv_buf[j, part, pl.ds(KEYS + which * PREFIX, PREFIX), :] = row[
-                    part, :, j * HD : (j + 1) * HD
+                    :, j * HD : (j + 1) * HD
                 ]
 
     def finish(j, due):
@@ -587,31 +558,27 @@
 
     @pl.when(live)
     def _():
-        for step in range(4):
-            down_copy(core, step).wait_send()
-        for step in range(3):
-            up_copy(core, step).wait_send()
-        for number, owner in ring_owners:
-            cross_copy(core, number, owner, pair).wait_send()
-        for hop in range(1, NX):
-            pick_copy(hop - 1, hop, sibling).wait_send()
-
-        @pl.when(~twin)
-        def _():
-            for number, owner in ring_owners:
-                for turn in range(2):
-                    sib_copy(turn, number, owner, core).wait_send()
+        for third in range(3):
+            for step in range(4):
+                down_copy(core, step, third).wait_send()
+            for step in range(3):
+                up_copy(core, step, third).wait_send()
+        for pair in range(2):
+            for hop in range(NX):
+                if pair + hop:
+                    pick_copy(0, core, pair, hop, sibling).wait_send()
 
         @pl.when(twin)
         def _():
-            for step in range(4):
-                down_copy(0, step).wait_send()
-            for step in range(3):
-                up_copy(0, step).wait_send()
-            for number, owner in ring_owners:
-                cross_copy(0, number, owner, pair).wait_send()
-            for col in range(NX):
-                pick_copy(NX - 1 + col, col, first_device).wait_send()
+            for third in range(3):
+                for step in range(4):
+                    down_copy(0, step, third).wait_send()
+                for step in range(3):
+                    up_copy(0, step, third).wait_send()
+            for pair in range(2):
+                for hop in range(NX):
+                    if pair + hop:
+                        pick_copy(1, 0, pair, hop, sibling).wait_send()
 
     for j in range(KVH):
         span = pl.ds(j * GROUPS * HD, GROUPS * HD)
@@ -638,8 +605,8 @@
             pltpu.VMEM((KVH, 2, SLOTS, HD), bf16),
             pltpu.VMEM((KVH, 2, T, HD), bf16),
             pltpu.VMEM((NY, 2, ROWS6, PREFIX, KVH * HD), bf16),
-            pltpu.VMEM((2 * NX - 1, 2, 2, PREFIX, KVH * HD), bf16),
-            pltpu.VMEM((NX, 2, 2, PREFIX, KVH * HD), bf16),
+            pltpu.VMEM((2, 2, NX, 2, PREFIX, KVH * HD), bf16),
+            pltpu.VMEM((2, NX, 2, PREFIX, KVH * HD), bf16),
             pltpu.VMEM((KVH, GROUPS, T, 2 * HD), jnp.float32),
             pltpu.VMEM((KVH, GROUPS, T, HD), jnp.float32),
             pltpu.VMEM((T, KEYS), jnp.float32),
@@ -651,14 +618,10 @@
             pltpu.SemaphoreType.DMA((KVH,)),
             pltpu.SemaphoreType.DMA((7, KVH)),
             pltpu.SemaphoreType.DMA((4, KVH)),
-            pltpu.SemaphoreType.DMA((2, 7)),
-            pltpu.SemaphoreType.DMA((2, 7)),
-            pltpu.SemaphoreType.DMA((2, 7)),
-            pltpu.SemaphoreType.DMA((2, 7)),
-            pltpu.SemaphoreType.DMA((2, 7)),
-            pltpu.SemaphoreType.DMA((2, 7)),
-            pltpu.SemaphoreType.DMA((2 * NX - 1,)),
-            pltpu.SemaphoreType.DMA((NX,)),
+            pltpu.SemaphoreType.DMA((2, 7, 3)),
+            pltpu.SemaphoreType.DMA((2, 7, 3)),
+            pltpu.SemaphoreType.DMA((2, 2, NX)),
+            pltpu.SemaphoreType.DMA((2, NX)),
             pltpu.SemaphoreType.REGULAR,
         ],
         compiler_params=pltpu.CompilerParams(

time: 40.7 us -> 39.9 us (0.980)
  the two profiles are of different devices: /device:TPU:4 before, /device:TPU:256 now
where the time goes in v5:
time: 39.9 us; the launch traced here: 39.7 us
  Pallas kernels  37.4 us (94%)
  local copies, waits for them, and re-layouts  2.29 us (6%)
    pallas_call x1, Pallas kernels, on_device(): pl.pallas_call(kernel, out_shape=jax.ShapeDtypeStruct((1, T, H * HD), bf1...  37.4 us
    unnamed x1, local copies, waits for them, and re-layouts  2.29 us

profile of v5, /device:TPU:256, one launch (start us, length us, event | category | flops | bytes accessed | tf_op | source)
XLA Modules:
  0.0 39.7 jit_solution(4892379184352784703)
XLA Ops:
  0.0 37.4 %shard_map.64 = bf16[1,128,4096]{2,1,0:T(8,128)(2,1)} custom-call(bf16[1,128,4096]{2,1,0:T(8,128)(2,1)} %q_hbm.1, bf16[2,1,128,512]{3,2,1,0:T(8,128)(2,1)} %kv_hbm.1, s32[1,512]{1,0:T(1,128)} %len_hbm.1, s32[1,512]{1,0:T(1,128)} %task_hbm.1, s32[192]{0:T(256)} %slot_smem.1, bf16[2,6,16,512]{3,2,1,0:T(8,128)(2,1)} %bank_hbm.1), custom_call_target="tpu_custom_call" | custom-call | tf_op jit(solution)/shard_map/pallas_call | solution.py:591
  37.4 2.3 %copy.8 = bf16[1,128,4096]{2,1,0:T(8,128)(2,1)} copy(bf16[1,128,4096]{2,1,0:T(8,128)(2,1)} %shard_map.64) | data formatting | bytes 2097152
